TPU v7x, 1024 devices: a whole 4x4x32 slice. The times are simulated.
1024 devices in a mesh: section: 64 (over z, core), tensor: 16 (over x, y).
Axes of the slice: x: 4, y: 4, z: 32, core: 2. Of those that a mesh axis runs over, the one named last changes fastest.
Arguments:
- section_inputs: bfloat16 [64, 2, 8192, 128], P('section', None, 'tensor'), may hold values from -6 to 6
- arriving_grad: bfloat16 [64, 8192, 128], P('section', 'tensor'), may hold values from -1.5 to 1.5
- loss_grad: bfloat16 [1, 8192, 128], P(None, 'tensor'), may hold values from -1.5 to 1.5
- factor_first: bfloat16 [64, 3, 64, 128, 128], P('section', None, 'tensor'), may hold values from -0.5 to 0.5
- factor_second: bfloat16 [64, 3, 64, 128, 128], P('section', None, 'tensor'), may hold values from -0.5 to 0.5
- gate_scales: float32 [64, 3, 8192], P('section', None, 'tensor'), may hold values from 0.25 to 1.5
- layer_count: int32 [64], P('section'), may hold values from 1 to 3, as said below
Outputs:
- last_emitted: bfloat16 [64, 8192, 128], P('section', 'tensor')
- factor_first_grad: bfloat16 [64, 3, 64, 128, 128], P('section', None, 'tensor')
- factor_second_grad: bfloat16 [64, 3, 64, 128, 128], P('section', None, 'tensor')
- gate_grad: float32 [64, 3, 8192], P('section', None, 'tensor')
Inputs may be any that keep to these rules, and one draw needn't show every extreme that they name: `layer_count`: every section runs at least one layer and some section runs 3.
All inputs are finite; a program needn't handle non-finite values.
Results may differ from a plain program's by a relative error of at most 0.017.
Values may be sent and summed in bfloat16 or wider, within the bound.
No kernel may reach another device: no remote copies, remote signals or barrier semaphores. Data moves between devices by JAX's collectives and lax.ppermute only.
A program may use at most 32 MiB of HBM per device.

v0:
```python
import jax
import jax.numpy as jnp
from jax import lax
from jax.sharding import PartitionSpec as P


def from_behind(value, axis, steps):
    count = lax.axis_size(axis)
    initial, last = (max(0, -steps), min(count, count - steps))
    return lax.ppermute(value, axis, [(source, source + steps) for source in range(initial, last)])


def permute_blocks(values):
    tensor_size = lax.axis_size("tensor")
    batch_count, local_blocks, block_size, token_count = values.shape
    blocks_all = local_blocks * tensor_size
    repeat_count = block_size // blocks_all
    shaped = values.reshape(
        batch_count, local_blocks, tensor_size, local_blocks, repeat_count, token_count
    )
    moved = lax.all_to_all(shaped, "tensor", split_axis=2, concat_axis=1, tiled=True)
    moved = moved.reshape(batch_count, blocks_all, local_blocks, repeat_count, token_count)
    return moved.transpose(0, 2, 3, 1, 4).reshape(
        batch_count, local_blocks, block_size, token_count
    )


def unpermute_blocks(values):
    tensor_size = lax.axis_size("tensor")
    local_blocks, block_size, token_count = values.shape
    blocks_all = local_blocks * tensor_size
    repeat_count = block_size // blocks_all
    shaped = values.reshape(local_blocks, repeat_count, tensor_size, local_blocks, token_count)
    moved = lax.all_to_all(shaped, "tensor", split_axis=2, concat_axis=0, tiled=True)
    moved = moved.reshape(blocks_all, repeat_count, local_blocks, token_count)
    return moved.transpose(2, 0, 1, 3).reshape(local_blocks, block_size, token_count)


def recompute(initial, factor_one, factor_two, gate_rows, layer_total):
    slot_count = factor_one.shape[0]
    hidden = initial
    saved = []
    for layer_slot in range(slot_count):
        first_out = jnp.einsum(
            "kij,mkjt->mkit", factor_one[layer_slot], hidden, preferred_element_type=jnp.float32
        ).astype(jnp.bfloat16)
        permuted = permute_blocks(first_out)
        mixed = jnp.einsum(
            "kij,mkjt->mkit", factor_two[layer_slot], permuted, preferred_element_type=jnp.float32
        )
        gate_now = gate_rows[layer_slot][None, :, :, None]
        next_hidden = (
            hidden.astype(jnp.float32) + gate_now * (mixed * jax.nn.sigmoid(mixed))
        ).astype(jnp.bfloat16)
        saved.append((hidden, permuted, mixed))
        hidden = jnp.where(layer_slot < layer_total, next_hidden, hidden)
    return saved


def shards(
    section_inputs, arriving_grad, loss_grad, factor_first, factor_second, gate_scales, layer_count
):
    moments = section_inputs.shape[1]
    slot_count = factor_first.shape[1]
    local_blocks = factor_first.shape[2]
    block_size = factor_first.shape[3]
    token_count = section_inputs.shape[3]
    first_local = factor_first[0]
    second_local = factor_second[0]
    gate_rows = gate_scales[0].reshape(slot_count, local_blocks, block_size)
    layer_total = layer_count[0]
    section_id = lax.axis_index("section")
    last_section = lax.axis_size("section") - 1
    inputs_local = section_inputs[0].reshape(moments, local_blocks, block_size, token_count)
    first_acc = [
        jnp.zeros((local_blocks, block_size, block_size), jnp.float32) for slot in range(slot_count)
    ]
    second_acc = [
        jnp.zeros((local_blocks, block_size, block_size), jnp.float32) for slot in range(slot_count)
    ]
    gate_acc = [jnp.zeros((local_blocks, block_size), jnp.float32) for slot in range(slot_count)]
    emitted = None
    for moment in range(moments):
        if moment == 0:
            arrived = arriving_grad[0].reshape(local_blocks, block_size, token_count)
        else:
            shifted = from_behind(emitted, "section", -1)
            from_loss = loss_grad[moment - 1].reshape(local_blocks, block_size, token_count)
            arrived = jnp.where(section_id == last_section, from_loss, shifted)
        computed = recompute(
            inputs_local[moment : moment + 1], first_local, second_local, gate_rows, layer_total
        )
        saved = [(record[0][0], record[1][0], record[2][0]) for record in computed]
        grad_now = arrived.astype(jnp.float32)
        for layer_slot in reversed(range(slot_count)):
            hidden, permuted, mixed = saved[layer_slot]
            is_live = layer_slot < layer_total
            logistic = jax.nn.sigmoid(mixed)
            gate_now = gate_rows[layer_slot][:, :, None]
            gate_term = jnp.sum(grad_now * (mixed * logistic), axis=2)
            gate_acc[layer_slot] = gate_acc[layer_slot] + jnp.where(
                is_live, gate_term, jnp.zeros_like(gate_term)
            )
            scaled = (grad_now * gate_now * logistic * (1.0 + mixed * (1.0 - logistic))).astype(
                jnp.bfloat16
            )
            backed = jnp.einsum(
                "kji,kjt->kit", second_local[layer_slot], scaled, preferred_element_type=jnp.float32
            ).astype(jnp.bfloat16)
            returned = unpermute_blocks(backed)
            moved_grad = grad_now + jnp.einsum(
                "kji,kjt->kit",
                first_local[layer_slot],
                returned,
                preferred_element_type=jnp.float32,
            )
            grad_now = jnp.where(is_live, moved_grad, grad_now)
            second_term = jnp.einsum(
                "kit,kjt->kij", scaled, permuted, preferred_element_type=jnp.float32
            )
            first_term = jnp.einsum(
                "kit,kjt->kij", returned, hidden, preferred_element_type=jnp.float32
            )
            second_acc[layer_slot] = second_acc[layer_slot] + jnp.where(
                is_live, second_term, jnp.zeros_like(second_term)
            )
            first_acc[layer_slot] = first_acc[layer_slot] + jnp.where(
                is_live, first_term, jnp.zeros_like(first_term)
            )
        emitted = grad_now.astype(jnp.bfloat16)
    last_emitted = emitted.reshape(1, local_blocks * block_size, token_count)
    gate_out = jnp.stack(gate_acc).reshape(1, slot_count, local_blocks * block_size)
    first_out = jnp.stack(first_acc).astype(jnp.bfloat16)[None]
    second_out = jnp.stack(second_acc).astype(jnp.bfloat16)[None]
    return (last_emitted, first_out, second_out, gate_out)


def solution(mesh):
    in_specs = (
        P("section", None, "tensor", None),
        P("section", "tensor", None),
        P(None, "tensor", None),
        P("section", None, "tensor", None, None),
        P("section", None, "tensor", None, None),
        P("section", None, "tensor"),
        P("section"),
    )
    out_specs = (
        P("section", "tensor", None),
        P("section", None, "tensor", None, None),
        P("section", None, "tensor", None, None),
        P("section", None, "tensor"),
    )
    return jax.shard_map(shards, mesh=mesh, in_specs=in_specs, out_specs=out_specs, check_vma=False)
```

profile of v0, /device:TPU:2, one launch (start us, length us, event | category | flops | bytes accessed | tf_op | source)
XLA Modules:
  0.0 179.7 jit_solution(2420558777227622007)
XLA Ops:
  0.6 1.0 fusion.168
  2.8 16.5 %all-to-all-start.6 = ((bf16[1,4,16,4,2,128]{5,1,4,3,0,2:T(4,128)(2,1)}), bf16[1,4,16,4,2,128]{5,1,4,3,0,2:T(4,128)(2,1)S(1)}, u32[]{:S(2)}, u32[]{:S(2)}) async-start(bf16[1,4,16,4,2,128]{5,1,4,3,0,2:T(4,128)(2,1)} %copy.185), calls=%async_computation.6 | async-start | bytes 262144 | tf_op jit(solution)/shard_map/all_to_all | solution.py:21
  21.2 4.9 %all-to-all-done.6 = bf16[1,4,16,4,2,128]{5,1,4,3,0,2:T(4,128)(2,1)S(1)} async-done(((bf16[1,4,16,4,2,128]{5,1,4,3,0,2:T(4,128)(2,1)}), bf16[1,4,16,4,2,128]{5,1,4,3,0,2:T(4,128)(2,1)S(1)}, u32[]{:S(2)}, u32[]{:S(2)}) %all-to-all-start.6) | async-done | bytes 131104 | tf_op jit(solution)/shard_map/all_to_all | solution.py:21
  26.1 5.1 %all-to-all-start = ((bf16[1,4,16,4,2,128]{5,1,4,3,0,2:T(4,128)(2,1)}), bf16[1,4,16,4,2,128]{5,1,4,3,0,2:T(4,128)(2,1)S(1)}, u32[]{:S(2)}, u32[]{:S(2)}) async-start(bf16[1,4,16,4,2,128]{5,1,4,3,0,2:T(4,128)(2,1)} %copy.151), calls=%async_computation | async-start | bytes 262144 | tf_op jit(solution)/shard_map/all_to_all | solution.py:21
  31.3 6.4 %all-to-all-done = bf16[1,4,16,4,2,128]{5,1,4,3,0,2:T(4,128)(2,1)S(1)} async-done(((bf16[1,4,16,4,2,128]{5,1,4,3,0,2:T(4,128)(2,1)}), bf16[1,4,16,4,2,128]{5,1,4,3,0,2:T(4,128)(2,1)S(1)}, u32[]{:S(2)}, u32[]{:S(2)}) %all-to-all-start) | async-done | bytes 131104 | tf_op jit(solution)/shard_map/all_to_all | solution.py:21
  38.0 1.0 fusion.106
  40.0 5.0 %all-to-all-start.1 = ((bf16[1,4,16,4,2,128]{5,1,4,3,0,2:T(4,128)(2,1)}), bf16[1,4,16,4,2,128]{5,1,4,3,0,2:T(4,128)(2,1)S(1)}, u32[]{:S(2)}, u32[]{:S(2)}) async-start(bf16[1,4,16,4,2,128]{5,1,4,3,0,2:T(4,128)(2,1)} %copy.156), calls=%async_computation.1 | async-start | bytes 262144 | tf_op jit(solution)/shard_map/all_to_all | solution.py:21
  46.0 5.4 %all-to-all-done.1 = bf16[1,4,16,4,2,128]{5,1,4,3,0,2:T(4,128)(2,1)S(1)} async-done(((bf16[1,4,16,4,2,128]{5,1,4,3,0,2:T(4,128)(2,1)}), bf16[1,4,16,4,2,128]{5,1,4,3,0,2:T(4,128)(2,1)S(1)}, u32[]{:S(2)}, u32[]{:S(2)}) %all-to-all-start.1) | async-done | bytes 131104 | tf_op jit(solution)/shard_map/all_to_all | solution.py:21
  51.4 5.1 %all-to-all-start.7 = ((bf16[1,4,16,4,2,128]{5,1,4,3,0,2:T(4,128)(2,1)}), bf16[1,4,16,4,2,128]{5,1,4,3,0,2:T(4,128)(2,1)S(1)}, u32[]{:S(2)}, u32[]{:S(2)}) async-start(bf16[1,4,16,4,2,128]{5,1,4,3,0,2:T(4,128)(2,1)} %copy.190), calls=%async_computation.7 | async-start | bytes 262144 | tf_op jit(solution)/shard_map/all_to_all | solution.py:21
  56.5 6.3 %all-to-all-done.7 = bf16[1,4,16,4,2,128]{5,1,4,3,0,2:T(4,128)(2,1)S(1)} async-done(((bf16[1,4,16,4,2,128]{5,1,4,3,0,2:T(4,128)(2,1)}), bf16[1,4,16,4,2,128]{5,1,4,3,0,2:T(4,128)(2,1)S(1)}, u32[]{:S(2)}, u32[]{:S(2)}) %all-to-all-start.7) | async-done | bytes 131104 | tf_op jit(solution)/shard_map/all_to_all | solution.py:21
  63.1 1.0 fusion.105
  65.2 5.1 %all-to-all-start.2 = ((bf16[1,4,16,4,2,128]{5,1,4,3,0,2:T(4,128)(2,1)}), bf16[1,4,16,4,2,128]{5,1,4,3,0,2:T(4,128)(2,1)S(1)}, u32[]{:S(2)}, u32[]{:S(2)}) async-start(bf16[1,4,16,4,2,128]{5,1,4,3,0,2:T(4,128)(2,1)} %copy.160), calls=%async_computation.2 | async-start | bytes 262144 | tf_op jit(solution)/shard_map/all_to_all | solution.py:21
  71.3 5.3 %all-to-all-done.2 = bf16[1,4,16,4,2,128]{5,1,4,3,0,2:T(4,128)(2,1)S(1)} async-done(((bf16[1,4,16,4,2,128]{5,1,4,3,0,2:T(4,128)(2,1)}), bf16[1,4,16,4,2,128]{5,1,4,3,0,2:T(4,128)(2,1)S(1)}, u32[]{:S(2)}, u32[]{:S(2)}) %all-to-all-start.2) | async-done | bytes 131104 | tf_op jit(solution)/shard_map/all_to_all | solution.py:21
  76.6 5.1 %all-to-all-start.8 = ((bf16[1,4,16,4,2,128]{5,1,4,3,0,2:T(4,128)(2,1)}), bf16[1,4,16,4,2,128]{5,1,4,3,0,2:T(4,128)(2,1)S(1)}, u32[]{:S(2)}, u32[]{:S(2)}) async-start(bf16[1,4,16,4,2,128]{5,1,4,3,0,2:T(4,128)(2,1)} %copy.194), calls=%async_computation.8 | async-start | bytes 262144 | tf_op jit(solution)/shard_map/all_to_all | solution.py:21
  82.8 5.3 %all-to-all-done.8 = bf16[1,4,16,4,2,128]{5,1,4,3,0,2:T(4,128)(2,1)S(1)} async-done(((bf16[1,4,16,4,2,128]{5,1,4,3,0,2:T(4,128)(2,1)}), bf16[1,4,16,4,2,128]{5,1,4,3,0,2:T(4,128)(2,1)S(1)}, u32[]{:S(2)}, u32[]{:S(2)}) %all-to-all-start.8) | async-done | bytes 131104 | tf_op jit(solution)/shard_map/all_to_all | solution.py:21
  89.9 5.1 %all-to-all-start.3 = ((bf16[4,2,16,4,128]{4,0,3,1,2:T(4,128)(2,1)}), bf16[4,2,16,4,128]{4,0,3,1,2:T(4,128)(2,1)S(1)}, u32[]{:S(2)}, u32[]{:S(2)}) async-start(bf16[4,2,16,4,128]{4,0,3,1,2:T(4,128)(2,1)} %copy.165), calls=%async_computation.3 | async-start | bytes 262144 | tf_op jit(solution)/shard_map/all_to_all | solution.py:34
  95.0 6.4 %all-to-all-done.3 = bf16[4,2,16,4,128]{4,0,3,1,2:T(4,128)(2,1)S(1)} async-done(((bf16[4,2,16,4,128]{4,0,3,1,2:T(4,128)(2,1)}), bf16[4,2,16,4,128]{4,0,3,1,2:T(4,128)(2,1)S(1)}, u32[]{:S(2)}, u32[]{:S(2)}) %all-to-all-start.3) | async-done | bytes 131104 | tf_op jit(solution)/shard_map/all_to_all | solution.py:34
  102.6 1.0 fusion.81
  104.6 5.1 %all-to-all-start.4 = ((bf16[4,2,16,4,128]{4,0,3,1,2:T(4,128)(2,1)}), bf16[4,2,16,4,128]{4,0,3,1,2:T(4,128)(2,1)S(1)}, u32[]{:S(2)}, u32[]{:S(2)}) async-start(bf16[4,2,16,4,128]{4,0,3,1,2:T(4,128)(2,1)} %copy.173), calls=%async_computation.4 | async-start | bytes 262144 | tf_op jit(solution)/shard_map/all_to_all | solution.py:34
  109.8 6.2 %all-to-all-done.4 = bf16[4,2,16,4,128]{4,0,3,1,2:T(4,128)(2,1)S(1)} async-done(((bf16[4,2,16,4,128]{4,0,3,1,2:T(4,128)(2,1)}), bf16[4,2,16,4,128]{4,0,3,1,2:T(4,128)(2,1)S(1)}, u32[]{:S(2)}, u32[]{:S(2)}) %all-to-all-start.4) | async-done | bytes 131104 | tf_op jit(solution)/shard_map/all_to_all | solution.py:34
  117.2 1.0 fusion.73
  119.2 5.1 %all-to-all-start.5 = ((bf16[4,2,16,4,128]{4,0,3,1,2:T(4,128)(2,1)}), bf16[4,2,16,4,128]{4,0,3,1,2:T(4,128)(2,1)S(1)}, u32[]{:S(2)}, u32[]{:S(2)}) async-start(bf16[4,2,16,4,128]{4,0,3,1,2:T(4,128)(2,1)} %copy.179), calls=%async_computation.5 | async-start | bytes 262144 | tf_op jit(solution)/shard_map/all_to_all | solution.py:34
  124.4 6.2 %all-to-all-done.5 = bf16[4,2,16,4,128]{4,0,3,1,2:T(4,128)(2,1)S(1)} async-done(((bf16[4,2,16,4,128]{4,0,3,1,2:T(4,128)(2,1)}), bf16[4,2,16,4,128]{4,0,3,1,2:T(4,128)(2,1)S(1)}, u32[]{:S(2)}, u32[]{:S(2)}) %all-to-all-start.5) | async-done | bytes 131104 | tf_op jit(solution)/shard_map/all_to_all | solution.py:34
  131.9 1.3 collective-permute-start
  133.4 1.7 collective-permute-done
  137.1 5.1 %all-to-all-start.9 = ((bf16[4,2,16,4,128]{4,0,3,1,2:T(4,128)(2,1)}), bf16[4,2,16,4,128]{4,0,3,1,2:T(4,128)(2,1)S(1)}, u32[]{:S(2)}, u32[]{:S(2)}) async-start(bf16[4,2,16,4,128]{4,0,3,1,2:T(4,128)(2,1)} %copy.199), calls=%async_computation.9 | async-start | bytes 262144 | tf_op jit(solution)/shard_map/all_to_all | solution.py:34
  142.3 6.2 %all-to-all-done.9 = bf16[4,2,16,4,128]{4,0,3,1,2:T(4,128)(2,1)S(1)} async-done(((bf16[4,2,16,4,128]{4,0,3,1,2:T(4,128)(2,1)}), bf16[4,2,16,4,128]{4,0,3,1,2:T(4,128)(2,1)S(1)}, u32[]{:S(2)}, u32[]{:S(2)}) %all-to-all-start.9) | async-done | bytes 131104 | tf_op jit(solution)/shard_map/all_to_all | solution.py:34
  149.5 1.0 fusion.55
  151.7 5.1 %all-to-all-start.10 = ((bf16[4,2,16,4,128]{4,0,3,1,2:T(4,128)(2,1)}), bf16[4,2,16,4,128]{4,0,3,1,2:T(4,128)(2,1)S(1)}, u32[]{:S(2)}, u32[]{:S(2)}) async-start(bf16[4,2,16,4,128]{4,0,3,1,2:T(4,128)(2,1)} %copy.206), calls=%async_computation.10 | async-start | bytes 262144 | tf_op jit(solution)/shard_map/all_to_all | solution.py:34
  157.0 6.1 %all-to-all-done.10 = bf16[4,2,16,4,128]{4,0,3,1,2:T(4,128)(2,1)S(1)} async-done(((bf16[4,2,16,4,128]{4,0,3,1,2:T(4,128)(2,1)}), bf16[4,2,16,4,128]{4,0,3,1,2:T(4,128)(2,1)S(1)}, u32[]{:S(2)}, u32[]{:S(2)}) %all-to-all-start.10) | async-done | bytes 131104 | tf_op jit(solution)/shard_map/all_to_all | solution.py:34
  165.9 5.1 %all-to-all-start.11 = ((bf16[4,2,16,4,128]{4,0,3,1,2:T(4,128)(2,1)}), bf16[4,2,16,4,128]{4,0,3,1,2:T(4,128)(2,1)S(1)}, u32[]{:S(2)}, u32[]{:S(2)}) async-start(bf16[4,2,16,4,128]{4,0,3,1,2:T(4,128)(2,1)} %copy.213), calls=%async_computation.11 | async-start | bytes 262144 | tf_op jit(solution)/shard_map/all_to_all | solution.py:34
  172.5 4.8 %all-to-all-done.11 = bf16[4,2,16,4,128]{4,0,3,1,2:T(4,128)(2,1)S(1)} async-done(((bf16[4,2,16,4,128]{4,0,3,1,2:T(4,128)(2,1)}), bf16[4,2,16,4,128]{4,0,3,1,2:T(4,128)(2,1)S(1)}, u32[]{:S(2)}, u32[]{:S(2)}) %all-to-all-start.11) | async-done | bytes 131104 | tf_op jit(solution)/shard_map/all_to_all | solution.py:34
  (126 shorter events, 27.2 us)
Async XLA Ops:
  0.6 1.1 copy-start.1
  2.8 23.3 %all-to-all-start.6 = ((bf16[1,4,16,4,2,128]{5,1,4,3,0,2:T(4,128)(2,1)}), bf16[1,4,16,4,2,128]{5,1,4,3,0,2:T(4,128)(2,1)S(1)}, u32[]{:S(2)}, u32[]{:S(2)}) async-start(bf16[1,4,16,4,2,128]{5,1,4,3,0,2:T(4,128)(2,1)} %copy.185), calls=%async_computation.6 | async-start | bytes 262144 | tf_op jit(solution)/shard_map/all_to_all | solution.py:21
  21.2 10.0 %copy-start.13 = (f32[1,3,512]{2,0,1:T(1,128)S(1)}, f32[1,3,512]{2,0,1:T(1,128)}, u32[]{:S(2)}) copy-start(f32[1,3,512]{2,0,1:T(1,128)} %param.12) | copy-start | bytes 18436
  21.2 16.5 %copy-start = (bf16[1,3,4,128,128]{4,3,2,1,0:T(8,128)(2,1)S(1)}, bf16[1,3,4,128,128]{4,3,2,1,0:T(8,128)(2,1)}, u32[]{:S(2)}) copy-start(bf16[1,3,4,128,128]{4,3,2,1,0:T(8,128)(2,1)} %param.11) | copy-start | bytes 1179652
  26.1 11.6 %all-to-all-start = ((bf16[1,4,16,4,2,128]{5,1,4,3,0,2:T(4,128)(2,1)}), bf16[1,4,16,4,2,128]{5,1,4,3,0,2:T(4,128)(2,1)S(1)}, u32[]{:S(2)}, u32[]{:S(2)}) async-start(bf16[1,4,16,4,2,128]{5,1,4,3,0,2:T(4,128)(2,1)} %copy.151), calls=%async_computation | async-start | bytes 262144 | tf_op jit(solution)/shard_map/all_to_all | solution.py:21
  31.2 6.8 %copy-start.14 = (f32[1,1,512]{2,0,1:T(1,128)}, f32[1,1,512]{2,0,1:T(1,128)S(1)}, u32[]{:S(2)}) copy-start(f32[1,1,512]{2,0,1:T(1,128)S(1)} %get-tuple-element.30) | copy-start | bytes 6148
  31.2 70.6 %copy-start.17 = (f32[1,1,512]{2,0,1:T(1,128)}, f32[1,1,512]{2,0,1:T(1,128)S(1)}, u32[]{:S(2)}) copy-start(f32[1,1,512]{2,0,1:T(1,128)S(1)} %get-tuple-element.29) | copy-start | bytes 6148
  38.0 1.0 copy-start.5
  40.0 11.4 %all-to-all-start.1 = ((bf16[1,4,16,4,2,128]{5,1,4,3,0,2:T(4,128)(2,1)}), bf16[1,4,16,4,2,128]{5,1,4,3,0,2:T(4,128)(2,1)S(1)}, u32[]{:S(2)}, u32[]{:S(2)}) async-start(bf16[1,4,16,4,2,128]{5,1,4,3,0,2:T(4,128)(2,1)} %copy.156), calls=%async_computation.1 | async-start | bytes 262144 | tf_op jit(solution)/shard_map/all_to_all | solution.py:21
  51.4 11.4 %all-to-all-start.7 = ((bf16[1,4,16,4,2,128]{5,1,4,3,0,2:T(4,128)(2,1)}), bf16[1,4,16,4,2,128]{5,1,4,3,0,2:T(4,128)(2,1)S(1)}, u32[]{:S(2)}, u32[]{:S(2)}) async-start(bf16[1,4,16,4,2,128]{5,1,4,3,0,2:T(4,128)(2,1)} %copy.190), calls=%async_computation.7 | async-start | bytes 262144 | tf_op jit(solution)/shard_map/all_to_all | solution.py:21
  63.1 1.0 copy-start.7
  65.2 11.4 %all-to-all-start.2 = ((bf16[1,4,16,4,2,128]{5,1,4,3,0,2:T(4,128)(2,1)}), bf16[1,4,16,4,2,128]{5,1,4,3,0,2:T(4,128)(2,1)S(1)}, u32[]{:S(2)}, u32[]{:S(2)}) async-start(bf16[1,4,16,4,2,128]{5,1,4,3,0,2:T(4,128)(2,1)} %copy.160), calls=%async_computation.2 | async-start | bytes 262144 | tf_op jit(solution)/shard_map/all_to_all | solution.py:21
  71.3 10.4 %copy-start.10 = (bf16[1,512,128]{2,1,0:T(8,128)(2,1)S(1)}, bf16[1,512,128]{2,1,0:T(8,128)(2,1)}, u32[]{:S(2)}) copy-start(bf16[1,512,128]{2,1,0:T(8,128)(2,1)} %param.9) | copy-start | bytes 393220
  76.6 11.4 %all-to-all-start.8 = ((bf16[1,4,16,4,2,128]{5,1,4,3,0,2:T(4,128)(2,1)}), bf16[1,4,16,4,2,128]{5,1,4,3,0,2:T(4,128)(2,1)S(1)}, u32[]{:S(2)}, u32[]{:S(2)}) async-start(bf16[1,4,16,4,2,128]{5,1,4,3,0,2:T(4,128)(2,1)} %copy.194), calls=%async_computation.8 | async-start | bytes 262144 | tf_op jit(solution)/shard_map/all_to_all | solution.py:21
  82.7 5.4 %copy-start.3 = (f32[4,128,128]{1,2,0:T(8,128)}, f32[4,128,128]{1,2,0:T(8,128)S(1)}, u32[]{:S(2)}) copy-start(f32[4,128,128]{1,2,0:T(8,128)S(1)} %copy.169) | copy-start | bytes 786436
  89.9 11.4 %all-to-all-start.3 = ((bf16[4,2,16,4,128]{4,0,3,1,2:T(4,128)(2,1)}), bf16[4,2,16,4,128]{4,0,3,1,2:T(4,128)(2,1)S(1)}, u32[]{:S(2)}, u32[]{:S(2)}) async-start(bf16[4,2,16,4,128]{4,0,3,1,2:T(4,128)(2,1)} %copy.165), calls=%async_computation.3 | async-start | bytes 262144 | tf_op jit(solution)/shard_map/all_to_all | solution.py:34
  101.5 1.0 copy-start.4
  101.6 1.0 copy-start.20
  104.6 11.4 %all-to-all-start.4 = ((bf16[4,2,16,4,128]{4,0,3,1,2:T(4,128)(2,1)}), bf16[4,2,16,4,128]{4,0,3,1,2:T(4,128)(2,1)S(1)}, u32[]{:S(2)}, u32[]{:S(2)}) async-start(bf16[4,2,16,4,128]{4,0,3,1,2:T(4,128)(2,1)} %copy.173), calls=%async_computation.4 | async-start | bytes 262144 | tf_op jit(solution)/shard_map/all_to_all | solution.py:34
  116.2 1.0 copy-start.19
  116.2 1.0 copy-start.22
  119.2 11.4 %all-to-all-start.5 = ((bf16[4,2,16,4,128]{4,0,3,1,2:T(4,128)(2,1)}), bf16[4,2,16,4,128]{4,0,3,1,2:T(4,128)(2,1)S(1)}, u32[]{:S(2)}, u32[]{:S(2)}) async-start(bf16[4,2,16,4,128]{4,0,3,1,2:T(4,128)(2,1)} %copy.179), calls=%async_computation.5 | async-start | bytes 262144 | tf_op jit(solution)/shard_map/all_to_all | solution.py:34
  130.7 1.0 copy-start.9
  131.9 3.2 %collective-permute-start = (bf16[4,128,128]{1,2,0:T(8,128)(2,1)S(1)}, bf16[4,128,128]{1,2,0:T(8,128)(2,1)S(1)}, u32[]{:S(2)}, u32[]{:S(2)}) collective-permute-start(bf16[4,128,128]{1,2,0:T(8,128)(2,1)S(1)} %fusion.18), channel_id=1, source_target_pairs={{16,0},{32,16},{48,32},{64,48},{80,64},{96,80},{112,96},{128,112},... | collective-permute-start | bytes 393224 | tf_op jit(solution)/shard_map/ppermute | solution.py:10
  137.1 11.4 %all-to-all-start.9 = ((bf16[4,2,16,4,128]{4,0,3,1,2:T(4,128)(2,1)}), bf16[4,2,16,4,128]{4,0,3,1,2:T(4,128)(2,1)S(1)}, u32[]{:S(2)}, u32[]{:S(2)}) async-start(bf16[4,2,16,4,128]{4,0,3,1,2:T(4,128)(2,1)} %copy.199), calls=%async_computation.9 | async-start | bytes 262144 | tf_op jit(solution)/shard_map/all_to_all | solution.py:34
  148.5 1.0 copy-start.8
  148.6 0.9 copy-start.12
  151.7 11.4 %all-to-all-start.10 = ((bf16[4,2,16,4,128]{4,0,3,1,2:T(4,128)(2,1)}), bf16[4,2,16,4,128]{4,0,3,1,2:T(4,128)(2,1)S(1)}, u32[]{:S(2)}, u32[]{:S(2)}) async-start(bf16[4,2,16,4,128]{4,0,3,1,2:T(4,128)(2,1)} %copy.206), calls=%async_computation.10 | async-start | bytes 262144 | tf_op jit(solution)/shard_map/all_to_all | solution.py:34
  163.3 1.0 copy-start.6
  163.3 0.9 copy-start.16
  163.3 1.0 copy-start.21
  165.9 11.4 %all-to-all-start.11 = ((bf16[4,2,16,4,128]{4,0,3,1,2:T(4,128)(2,1)}), bf16[4,2,16,4,128]{4,0,3,1,2:T(4,128)(2,1)S(1)}, u32[]{:S(2)}, u32[]{:S(2)}) async-start(bf16[4,2,16,4,128]{4,0,3,1,2:T(4,128)(2,1)} %copy.213), calls=%async_computation.11 | async-start | bytes 262144 | tf_op jit(solution)/shard_map/all_to_all | solution.py:34
  (4 other events, 3.3 us)
where the time goes:
time: 181 us; the launch traced here: 180 us
  starting transfers between devices  73.4 us (41%)
  waiting for transfers between devices  71.3 us (39%)
  local copies, waits for them, and re-layouts  20.5 us (11%)
  matrix products  11.7 us (6%)
  between operations  1.91 us (1%)
    all_to_all x6, starting transfers between devices, permute_blocks(): lax.all_to_all(shaped, 'tensor', split_axis=2, concat_axis=1, tiled=True)  41.8 us
    all_to_all x6, waiting for transfers between devices, unpermute_blocks(): lax.all_to_all(shaped, 'tensor', split_axis=2, concat_axis=0, tiled=True)  36 us
    all_to_all x6, waiting for transfers between devices, permute_blocks(): lax.all_to_all(shaped, 'tensor', split_axis=2, concat_axis=1, tiled=True)  33.6 us
    all_to_all x6, starting transfers between devices, unpermute_blocks(): lax.all_to_all(shaped, 'tensor', split_axis=2, concat_axis=0, tiled=True)  30.3 us
    unnamed x48, local copies, waits for them, and re-layouts  7.08 us
    reshape x6, local copies, waits for them, and re-layouts, permute_blocks(): values.reshape(batch_count, local_blocks, tensor_size, local_blocks, repe...  4.98 us
    reshape x6, local copies, waits for them, and re-layouts, unpermute_blocks(): values.reshape(local_blocks, repeat_count, tensor_size, local_blocks, tok...  4.56 us
    dot_general x6, matrix products, shards(): jnp.einsum('kji,kjt->kit', first_local[layer_slot], returned, preferred_e...  3.72 us
  transfers between devices with their start and end apart: 13, of which 13 were waited for; matrix products, arithmetic and copies ran while one was open for 4% of the time, Pallas kernels for 0%

commit v1 on v0

v1 whole, which is shorter than its diff:
```python
import jax
import jax.numpy as jnp
from jax import lax
from jax.experimental import pallas as pl
from jax.experimental.pallas import tpu as pltpu
from jax.sharding import PartitionSpec as P

F32 = jnp.float32
BF16 = jnp.bfloat16


def call(body, name, h_in=(), v_in=(), pins=(), v_out=(), h_out=(), into=(), chain=False):
    vmem = pl.BlockSpec(memory_space=pltpu.VMEM)
    hbm = pl.BlockSpec(memory_space=pltpu.HBM)
    arrays = [item[0] if isinstance(item, tuple) else item for item in h_in]
    places = [item[1] if isinstance(item, tuple) else () for item in h_in]
    shapes = [item[0] if isinstance(item, tuple) else item for item in h_out]
    targets = [item[1] if isinstance(item, tuple) else () for item in h_out]
    loads = [pltpu.VMEM(a.shape[len(p) :], a.dtype) for a, p in zip(arrays, places)]
    stores = [pltpu.VMEM(a.shape[len(p) :], a.dtype) for a, p in zip(shapes, targets)]
    pins = [*pins, *(array for _, array in into)]
    ahead = len(arrays) + len(v_in) + len(pins) - len(into)
    alias = {ahead + k: len(v_out) + number for k, (number, _) in enumerate(into)}
    arrays = [pltpu.with_memory_space_constraint(a, pltpu.HBM) for a in arrays]
    pins = [pltpu.with_memory_space_constraint(a, pltpu.HBM) for a in pins]
    inputs = (*arrays, *v_in, *pins)

    def at(ref, place):
        return ref.at[place] if place else ref

    def kernel(*refs):
        sources, refs = refs[: len(arrays)], refs[len(arrays) :]
        views, refs = refs[: len(v_in)], refs[len(v_in) + len(pins) :]
        results, refs = refs[: len(v_out)], refs[len(v_out) :]
        sinks, refs = refs[: len(shapes)], refs[len(shapes) :]
        loaded, refs = refs[: len(loads)], refs[len(loads) :]
        staged, refs = refs[: len(stores)], refs[len(stores) :]
        in_sems, out_sems = refs
        copies = [
            pltpu.make_async_copy(at(source, place), buffer, in_sems.at[number])
            for number, (source, place, buffer) in enumerate(zip(sources, places, loaded))
        ]
        for copy in copies:
            copy.start()
        pending = []

        def emit(number, value, ref=None):
            if ref is None:
                ref = staged[number]
                ref[...] = value
            copy = pltpu.make_async_copy(ref, at(sinks[number], targets[number]), out_sems.at[number])
            copy.start()
            pending.append(copy)

        waited = set()

        def load(number):
            if number not in waited:
                waited.add(number)
                copies[number].wait()
            return loaded[number]

        body(emit, load, views, results)
        for copy in pending:
            copy.wait()

    moved = sum(a.size * a.dtype.itemsize for a in (*arrays, *v_in, *v_out, *shapes))
    moved = moved if chain else 1024
    return pl.pallas_call(
        kernel,
        out_shape=[*v_out, *(pltpu.HBM(a.shape, a.dtype) for a in shapes)],
        in_specs=[hbm] * len(arrays) + [vmem] * len(v_in) + [hbm] * len(pins),
        out_specs=[vmem] * len(v_out) + [hbm] * len(shapes),
        scratch_shapes=[
            *loads,
            *stores,
            pltpu.SemaphoreType.DMA((max(1, len(loads)),)),
            pltpu.SemaphoreType.DMA((max(1, len(stores)),)),
        ],
        input_output_aliases=alias,
        name=name,
        compiler_params=pltpu.CompilerParams(vmem_limit_bytes=16 << 20),
        cost_estimate=pl.CostEstimate(flops=0, bytes_accessed=moved, transcendentals=0),
    )(*inputs)


def merged(name, tasks, pins=()):
    sources, keys, plans = [], {}, []
    v_out, h_out, into = [], [], []
    for body, needs, shows, keeps, fills in tasks:
        numbers = []
        for item in needs:
            array, place = item if isinstance(item, tuple) else (item, ())
            key = (id(array), place)
            if key not in keys:
                keys[key] = len(sources)
                sources.append((array, place))
            numbers.append(keys[key])
        plans.append((body, numbers, len(v_out), len(h_out)))
        into += [(number + len(h_out), array) for number, array in fills]
        v_out += shows
        h_out += keeps

    def kernel(emit, load, views, results):
        for body, numbers, shown, kept in plans:
            body(
                lambda number, value: emit(kept + number, value),
                lambda number: load(numbers[number]),
                views,
                results[shown:],
            )

    outs = call(kernel, name, h_in=sources, pins=pins, v_out=v_out, h_out=h_out, into=into)
    split = []
    for (_, _, shown, kept), (_, _, shows, keeps, _) in zip(plans, tasks):
        base = len(v_out) + kept
        split.append([*outs[shown : shown + len(shows)], *outs[base : base + len(keeps)]])
    return split


def dot(left, right):
    return jnp.dot(left, right, preferred_element_type=F32)


def dot_t(left, right):
    return lax.dot_general(left, right, (((1,), (1,)), ((), ())), preferred_element_type=F32)


def one_hot(match):
    return jnp.where(match, 1.0, 0.0).astype(BF16)


def first_rows(sizes, axis):
    blocks, size, parts = sizes
    rows = blocks * size
    each = size // parts
    wire = lax.broadcasted_iota(jnp.int32, (rows, rows), axis)
    natural = lax.broadcasted_iota(jnp.int32, (rows, rows), 1 - axis)
    part = wire // (blocks * each)
    block = (wire // each) % blocks
    return one_hot(natural == block * size + part * each + wire % each)


def second_rows(sizes, axis):
    blocks, size, parts = sizes
    rows = blocks * size
    every = blocks * parts
    repeat = size // every
    wire = lax.broadcasted_iota(jnp.int32, (rows, rows), axis)
    natural = lax.broadcasted_iota(jnp.int32, (rows, rows), 1 - axis)
    source = wire // (blocks * repeat)
    block = (wire // repeat) % blocks
    return one_hot(natural == block * size + (wire % repeat) * every + source)


def sigmoid(values):
    return 1.0 / (1.0 + jnp.exp(-values))


def first_wire(sizes, factor):
    blocks, size, _ = sizes
    order = first_rows(sizes, 0)
    return [
        dot(order[:, block * size : (block + 1) * size], factor[block]).astype(BF16)
        for block in range(blocks)
    ]


def first_back(sizes, factor):
    blocks, size, _ = sizes
    order = first_rows(sizes, 1)
    return [
        dot(
            factor[block].astype(F32).T.astype(BF16), order[block * size : (block + 1) * size]
        ).astype(BF16)
        for block in range(blocks)
    ]


def second_wire(sizes, factor):
    blocks, size, _ = sizes
    order = second_rows(sizes, 1)
    return [
        dot(factor[block], order[block * size : (block + 1) * size]).astype(BF16)
        for block in range(blocks)
    ]


def second_back(sizes, factor):
    blocks, size, _ = sizes
    order = second_rows(sizes, 0)
    return [
        dot(
            order[:, block * size : (block + 1) * size], factor[block].astype(F32).T.astype(BF16)
        ).astype(BF16)
        for block in range(blocks)
    ]


def put_rows(ref, parts):
    size = parts[0].shape[0]
    for number, part in enumerate(parts):
        ref[number * size : (number + 1) * size, :] = part


def put_columns(ref, parts):
    size = parts[0].shape[1]
    for number, part in enumerate(parts):
        ref[:, number * size : (number + 1) * size] = part


def column(row, lanes):
    return jnp.broadcast_to(row, (lanes, row.shape[1])).T


def both(value):
    return jnp.concatenate([value, value], axis=1)


def branch_of(mixed):
    return mixed * sigmoid(mixed)


def slope_of(mixed, gates):
    logistic = sigmoid(mixed)
    return gates * logistic * (1.0 + mixed * (1.0 - logistic))


def exchange(values, parts):
    rows, columns = values.shape
    shaped = values.reshape(parts, rows // parts, columns)
    return lax.all_to_all(shaped, "tensor", 0, 0, tiled=True).reshape(rows, columns)


def shards(
    section_inputs, arriving_grad, loss_grad, factor_first, factor_second, gate_scales, layer_count
):
    slots, blocks, size = factor_first.shape[1:4]
    tokens = section_inputs.shape[3]
    parts = lax.axis_size("tensor")
    sizes = (blocks, size, parts)
    rows = blocks * size
    live = jnp.arange(slots) < layer_count[0]
    gate = jnp.where(live[:, None], gate_scales[0], 0.0)[:, None]
    alive = jnp.where(live[:, None], jnp.ones_like(gate_scales[0]), 0.0)[:, None]
    sections = lax.axis_size("section")
    is_last = lax.axis_index("section") == sections - 1
    loss = jnp.where(is_last, loss_grad[0], jnp.zeros_like(loss_grad[0]))
    last = slots - 1

    def shape(columns, dtype=BF16):
        return jax.ShapeDtypeStruct((rows, columns), dtype)

    wide, slim, square = shape(2 * tokens), shape(tokens), shape(rows)
    wide_f32, slim_f32 = shape(2 * tokens, F32), shape(tokens, F32)
    factor_shape = jax.ShapeDtypeStruct(factor_first.shape, BF16)

    def first_of(slot):
        return (factor_first, (0, slot))

    def second_of(slot):
        return (factor_second, (0, slot))

    def gate_of(slot):
        return (gate, (slot,))

    def open_chain(emit, load, views, results):
        order = first_rows(sizes, 0)
        factor, inputs = load(0), load(1)
        hidden = jnp.concatenate([inputs[0], inputs[1]], axis=1)
        natural = jnp.concatenate(
            [
                dot(factor[block], hidden[block * size : (block + 1) * size]).astype(BF16)
                for block in range(blocks)
            ],
            axis=0,
        )
        emit(0, dot(order, natural).astype(BF16))

    (send,) = call(
        open_chain, "open", h_in=[first_of(0), (section_inputs, (0,))], h_out=[wide], chain=True
    )
    started = section_inputs

    wires, hiddens, mixeds = [], [], []
    for slot in range(last):

        def prepare(emit, load, views, results, slot=slot):
            put_rows(results[0], second_wire(sizes, load(0)))
            put_columns(results[1], first_wire(sizes, load(1)))
            results[2][...] = column(load(2)[...], tokens)
            before = load(3)
            if slot == 0:
                results[3][...] = jnp.concatenate([before[0], before[1]], axis=1)
            else:
                results[3][...] = before[...]

        second_now, first_now, gate_now, hidden = call(
            prepare,
            f"prepare_forward_{slot}",
            h_in=[
                second_of(slot),
                first_of(slot + 1),
                gate_of(slot),
                (section_inputs, (0,)) if slot == 0 else hiddens[-1],
            ],
            pins=[started],
            v_out=[square, square, slim_f32, wide],
        )

        def forward(emit, load, views, results):
            received, hidden, gate_now, second_now, first_now = views
            emit(1, None, received)
            mixed = dot(second_now[...], received[...])
            emit(2, mixed)
            fresh = (hidden[...].astype(F32) + both(gate_now[...]) * branch_of(mixed)).astype(BF16)
            emit(3, fresh)
            emit(0, dot(first_now[...], fresh).astype(BF16))

        send, wire, mixed, fresh = call(
            forward,
            f"forward_{slot}",
            v_in=[exchange(send, parts), hidden, gate_now, second_now, first_now],
            h_out=[wide, wide, wide_f32, wide],
            chain=True,
        )
        wires.append(wire)
        mixeds.append(mixed)
        hiddens.append(fresh)
        started = fresh

    def prepare_turn(emit, load, views, results):
        second = load(0)
        put_rows(results[0], second_wire(sizes, second))
        put_columns(results[1], second_back(sizes, second))
        results[2][...] = column(load(1)[...], tokens)
        results[3][...] = load(2)[...]

    second_now, back_now, gate_now, arriving = call(
        prepare_turn,
        "prepare_turn",
        h_in=[second_of(last), gate_of(last), (arriving_grad, (0,))],
        pins=[started],
        v_out=[square, square, slim_f32, slim],
    )

    def turn(emit, load, views, results):
        received, arriving, gate_now, second_now, back_now = views
        emit(1, None, received)
        mixed = dot(second_now[...], received[...])
        emit(2, mixed)
        slope = slope_of(mixed[:, :tokens], gate_now[...])
        scaled = (arriving[...].astype(F32) * slope).astype(BF16)
        emit(3, scaled)
        emit(0, dot(back_now[...], scaled).astype(BF16))

    send, wire, mixed, scaled = call(
        turn,
        "turn",
        v_in=[exchange(send, parts), arriving, gate_now, second_now, back_now],
        h_out=[slim, wide, wide_f32, slim],
        chain=True,
    )
    wires.append(wire)
    mixeds.append(mixed)
    started = scaled

    scaleds = [[None] * slots, [None] * slots]
    grads = [[None] * slots, [None] * slots]
    returns = [[None] * slots, [None] * slots]
    scaleds[0][last], grads[0][last] = scaled, (arriving_grad, (0,))
    gate_shape = jax.ShapeDtypeStruct(gate.shape, F32)

    def gate_sums(slot, filled):
        def body(emit, load, views, results):
            branch = branch_of(load(0)[...])
            terms = load(1)[...].astype(F32) * branch[:, :tokens]
            terms += load(2)[...].astype(F32) * branch[:, tokens:]
            sums = jnp.sum(terms.T, axis=0, keepdims=True)
            emit(0, jnp.where(load(3)[...] > 0, sums, 0.0))

        return (
            body,
            [mixeds[slot], grads[0][slot], grads[1][slot], (alive, (slot,))],
            [],
            [(gate_shape, (slot,))],
            [] if filled is None else [(0, filled)],
        )

    def second_sums(slot, filled):
        def body(emit, load, views, results):
            order = second_rows(sizes, 1)
            natural = dot(order, load(0)[...]).astype(BF16)
            scaled = jnp.concatenate([load(1)[...], load(2)[...]], axis=1)
            sums = []
            for block in range(blocks):
                span = slice(block * size, (block + 1) * size)
                sums.append(dot_t(scaled[span], natural[span]).astype(BF16))
            emit(0, jnp.stack(sums))

        return (
            body,
            [wires[slot], scaleds[0][slot], scaleds[1][slot]],
            [],
            [(factor_shape, (0, slot))],
            [] if filled is None else [(0, filled)],
        )

    def first_sum(earlier, later, hidden):
        wire = jnp.concatenate([earlier, later], axis=1)
        natural = dot(first_rows(sizes, 1), wire).astype(BF16)
        sums = []
        for block in range(blocks):
            span = slice(block * size, (block + 1) * size)
            sums.append(dot_t(natural[span], hidden[span]).astype(BF16))
        return jnp.stack(sums)

    def first_sums(slot, filled):
        def body(emit, load, views, results):
            emit(0, first_sum(load(0)[...], load(1)[...], load(2)[...]))

        return (
            body,
            [returns[0][slot], returns[1][slot], hiddens[slot - 1]],
            [],
            [(factor_shape, (0, slot))],
            [] if filled is None else [(0, filled)],
        )

    def step(moment, slot, send, started, tasks=()):
        columns = slice(moment * tokens, (moment + 1) * tokens)
        kept = BF16 if slot + 1 == last else F32

        def prepare(emit, load, views, results):
            put_rows(results[0], first_back(sizes, load(0)))
            put_columns(results[1], second_back(sizes, load(1)))
            gates = column(load(2)[...], tokens)
            results[2][...] = slope_of(load(3)[:, columns], gates)
            results[3][...] = load(4)[...]

        task = (
            prepare,
            [
                first_of(slot + 1),
                second_of(slot),
                gate_of(slot),
                mixeds[slot],
                grads[moment][slot + 1],
            ],
            [square, square, slim_f32, shape(tokens, kept)],
            [],
            [],
        )
        ready, *others = merged(f"window_{moment}_{slot}", [task, *tasks], [started])
        first_now, second_now, slope, grad = ready

        def backward(emit, load, views, results):
            received, grad, slope, first_now, second_now = views
            emit(1, None, received)
            grad_now = grad[...].astype(F32) + dot(first_now[...], received[...])
            emit(3, grad_now)
            scaled = (grad_now * slope[...]).astype(BF16)
            emit(2, scaled)
            emit(0, dot(second_now[...], scaled).astype(BF16))

        send, returned, scaled, grad = call(
            backward,
            f"backward_{moment}_{slot}",
            v_in=[exchange(send, parts), grad, slope, first_now, second_now],
            h_out=[slim, slim, slim, slim_f32],
            chain=True,
        )
        returns[moment][slot + 1] = returned
        scaleds[moment][slot] = scaled
        grads[moment][slot] = grad
        return send, scaled, others

    for slot in reversed(range(last)):
        send, started, _ = step(0, slot, send, started)

    def prepare_emit(emit, load, views, results):
        put_rows(results[0], first_back(sizes, load(0)))
        results[1][...] = load(1)[...]

    def prepare_again(emit, load, views, results):
        put_columns(results[0], second_back(sizes, load(0)))
        gates = column(load(1)[...], tokens)
        results[1][...] = slope_of(load(2)[:, tokens:], gates)
        results[2][...] = load(3)[...]

    (first_now, grad), (second_now, slope, loss) = merged(
        "window_emit",
        [
            (prepare_emit, [first_of(0), grads[0][0]], [square, slim_f32], [], []),
            (
                prepare_again,
                [second_of(last), gate_of(last), mixeds[last], loss],
                [square, slim_f32, slim],
                [],
                [],
            ),
        ],
        [started],
    )

    def emit_grad(emit, load, views, results):
        received, grad, first_now = views[:3]
        emit(0, None, received)
        results[0][...] = (grad[...] + dot(first_now[...], received[...])).astype(BF16)

    emitted, returns[0][0] = call(
        emit_grad,
        "emit",
        v_in=[exchange(send, parts), grad, first_now, loss],
        v_out=[slim],
        h_out=[slim],
        chain=True,
    )
    shifted = lax.ppermute(
        emitted, "section", [(source, source - 1) for source in range(1, sections)]
    )

    def again(emit, load, views, results):
        shifted, loss, slope, second_now = views
        grad_now = shifted[...].astype(F32) + loss[...].astype(F32)
        emit(2, grad_now.astype(BF16))
        scaled = (grad_now * slope[...]).astype(BF16)
        emit(1, scaled)
        emit(0, dot(second_now[...], scaled).astype(BF16))

    send, scaleds[1][last], grads[1][last] = call(
        again,
        "again",
        v_in=[shifted, loss, slope, second_now],
        h_out=[slim, slim, slim],
        chain=True,
    )
    started = scaleds[1][last]

    gate_out, second_out, first_out = None, None, None
    for slot in reversed(range(last)):
        tasks = [gate_sums(slot + 1, gate_out), second_sums(slot + 1, second_out)]
        if slot + 2 < slots:
            tasks.append(first_sums(slot + 2, first_out))
        send, started, others = step(1, slot, send, started, tasks)
        (gate_out,), (second_out,) = others[:2]
        if slot + 2 < slots:
            ((first_out,),) = others[2:]

    def prepare_close(emit, load, views, results):
        put_rows(results[0], first_back(sizes, load(0)))
        results[1][...] = load(1)[...]
        results[2][...] = load(2)[...]
        inputs = load(3)
        results[3][...] = jnp.concatenate([inputs[0], inputs[1]], axis=1)

    task = (
        prepare_close,
        [first_of(0), grads[1][0], returns[0][0], (section_inputs, (0,))],
        [square, slim_f32, slim, wide],
        [],
        [],
    )
    (first_now, grad, earlier, hidden), (gate_out,), (second_out,), (first_out,) = merged(
        "window_close",
        [task, gate_sums(0, gate_out), second_sums(0, second_out), first_sums(1, first_out)],
        [started],
    )

    def close(emit, load, views, results):
        received, grad, first_now, earlier, hidden = views
        emit(0, (grad[...] + dot(first_now[...], received[...])).astype(BF16))
        emit(1, first_sum(earlier[...], received[...], hidden[...]))

    emitted, first_out = call(
        close,
        "close",
        v_in=[exchange(send, parts), grad, first_now, earlier, hidden],
        h_out=[slim, (factor_shape, (0, 0))],
        into=[(1, first_out)],
        chain=True,
    )
    return emitted[None], first_out, second_out, gate_out.reshape(gate_scales.shape)


def solution(mesh):
    in_specs = (
        P("section", None, "tensor", None),
        P("section", "tensor", None),
        P(None, "tensor", None),
        P("section", None, "tensor", None, None),
        P("section", None, "tensor", None, None),
        P("section", None, "tensor"),
        P("section"),
    )
    out_specs = (
        P("section", "tensor", None),
        P("section", None, "tensor", None, None),
        P("section", None, "tensor", None, None),
        P("section", None, "tensor"),
    )
    return jax.shard_map(shards, mesh=mesh, in_specs=in_specs, out_specs=out_specs, check_vma=False)
```

time: 181 us -> 139 us (0.77)
  Pallas kernels: 0 us -> 38.8 us
  waiting for transfers between devices: 71.3 us -> 35.4 us
  local copies, waits for them, and re-layouts: 20.5 us -> 0.68 us
  starting transfers between devices: 73.4 us -> 60.3 us
  matrix products: 11.7 us -> 0 us
    pallas_call x0 -> x20, Pallas kernels: none -> 38.8 us  [call(): pl.pallas_call(kernel, out_shape=[*v_out, *(pltpu.HBM(a.shape, a.dtype) f...]
    all_to_all x12 -> x9, waiting for transfers between devices: 69.5 us -> 33.5 us  [exchange(): lax.all_to_all(shaped, 'tensor', 0, 0, tiled=True).reshape(rows, columns)]
    all_to_all x12 -> x9, starting transfers between devices: 72.1 us -> 59 us  [exchange(): lax.all_to_all(shaped, 'tensor', 0, 0, tiled=True).reshape(rows, columns)]
    dot_general x36 -> x0, matrix products: 11.7 us -> none  [the longest x6 3.72 us: shards(): jnp.einsum('kji,kjt->kit', first_local[layer_slot], returned, preferred_e...]
    reshape x12 -> x0, local copies, waits for them, and re-layouts: 9.54 us -> none  [the longest x6 4.98 us: permute_blocks(): values.reshape(batch_count, local_blocks, tensor_size, local_blocks, repe...]
    unnamed x48 -> x4, local copies, waits for them, and re-layouts: 7.08 us -> 0.01 us
  transfers between devices with their start and end apart: 13 -> 10, of which waited for: 13 -> 10; matrix products, arithmetic and copies ran while one was open for 4% -> 1% of each run, Pallas kernels for 0% -> 17%
where the time goes in v1:
time: 139 us; the launch traced here: 138 us
  starting transfers between devices  60.3 us (43%)
  Pallas kernels  38.8 us (28%)
  waiting for transfers between devices  35.4 us (25%)
  between operations  1.65 us (1%)
    all_to_all x9, starting transfers between devices, exchange(): lax.all_to_all(shaped, 'tensor', 0, 0, tiled=True).reshape(rows, columns)  59 us
    pallas_call x20, Pallas kernels, call(): pl.pallas_call(kernel, out_shape=[*v_out, *(pltpu.HBM(a.shape, a.dtype) f...  38.8 us
    all_to_all x9, waiting for transfers between devices, exchange(): lax.all_to_all(shaped, 'tensor', 0, 0, tiled=True).reshape(rows, columns)  33.5 us
  transfers between devices with their start and end apart: 10, of which 10 were waited for; matrix products, arithmetic and copies ran while one was open for 1% of the time, Pallas kernels for 17%

profile of v1, /device:TPU:2, one launch (start us, length us, event | category | flops | bytes accessed | tf_op | source)
XLA Modules:
  0.0 138.2 jit_solution(2749481007729021786)
XLA Ops:
  0.6 2.2 %open.1 = bf16[512,256]{1,0:T(8,128)(2,1)} custom-call(bf16[1,3,4,128,128]{4,3,2,1,0:T(8,128)(2,1)} %refs_0_.19, bf16[1,2,512,128]{3,2,1,0:T(8,128)(2,1)} %refs_3_.3), custom_call_target="tpu_custom_call" | custom-call | bytes 917504 | tf_op jit(solution)/shard_map/open/pallas_call | solution.py:69
  2.9 16.5 %all-to-all-start = ((bf16[16,32,256]{2,1,0:T(8,128)(2,1)}), bf16[16,32,256]{2,1,0:T(8,128)(2,1)S(1)}, u32[]{:S(2)}, u32[]{:S(2)}) async-start(bf16[16,32,256]{2,1,0:T(8,128)(2,1)} %bitcast.36), calls=%async_computation | async-start | bytes 524288 | tf_op jit(solution)/shard_map/all_to_all | solution.py:232
  20.8 1.8 %prepare_forward_0.1 = (bf16[512,512]{1,0:T(8,128)(2,1)S(1)}, bf16[512,512]{1,0:T(8,128)(2,1)S(1)}, f32[512,128]{1,0:T(8,128)S(1)}, bf16[512,256]{1,0:T(8,128)(2,1)S(1)}) custom-call(bf16[1,3,4,128,128]{4,3,2,1,0:T(8,128)(2,1)} %refs_1_.13, bf16[1,3,4,128,128]{4,3,2,1,0:T(8,128)(2,1)} %refs_0_.19, f32[3,1,512]{2,1,0:T(1,128)} %broadcast_select_fusion.refs_2_.refs_1_.refs_3_, ...), custom_call_target="tpu_custom_call" | custom-call | bytes 1024 | tf_op jit(solution)/shard_map/prepare_forward_0/pallas_call | solution.py:69
  22.5 4.0 %all-to-all-done = bf16[16,32,256]{2,1,0:T(8,128)(2,1)S(1)} async-done(((bf16[16,32,256]{2,1,0:T(8,128)(2,1)}), bf16[16,32,256]{2,1,0:T(8,128)(2,1)S(1)}, u32[]{:S(2)}, u32[]{:S(2)}) %all-to-all-start) | async-done | bytes 262176 | tf_op jit(solution)/shard_map/all_to_all | solution.py:232
  26.5 1.5 %forward_0.1 = (bf16[512,256]{1,0:T(8,128)(2,1)}, bf16[512,256]{1,0:T(8,128)(2,1)}, f32[512,256]{1,0:T(8,128)}, bf16[512,256]{1,0:T(8,128)(2,1)}) custom-call(bf16[512,256]{1,0:T(8,128)(2,1)S(1)} %bitcast.27, bf16[512,256]{1,0:T(8,128)(2,1)S(1)} %get-tuple-element.84.refs_1_, f32[512,128]{1,0:T(8,128)S(1)} %get-tuple-element.85.refs_2_, ...), custom_call_target="tpu_custom_call" | custom-call | bytes 3145728 | tf_op jit(solution)/shard_map/forward_0/pallas_call | solution.py:69
  28.0 5.2 %all-to-all-start.1 = ((bf16[16,32,256]{2,1,0:T(8,128)(2,1)}), bf16[16,32,256]{2,1,0:T(8,128)(2,1)S(1)}, u32[]{:S(2)}, u32[]{:S(2)}) async-start(bf16[16,32,256]{2,1,0:T(8,128)(2,1)} %bitcast.37), calls=%async_computation.1 | async-start | bytes 524288 | tf_op jit(solution)/shard_map/all_to_all | solution.py:232
  33.2 1.7 %prepare_forward_1.1 = (bf16[512,512]{1,0:T(8,128)(2,1)S(1)}, bf16[512,512]{1,0:T(8,128)(2,1)S(1)}, f32[512,128]{1,0:T(8,128)S(1)}, bf16[512,256]{1,0:T(8,128)(2,1)S(1)}) custom-call(bf16[1,3,4,128,128]{4,3,2,1,0:T(8,128)(2,1)} %refs_1_.13, bf16[1,3,4,128,128]{4,3,2,1,0:T(8,128)(2,1)} %refs_0_.19, f32[3,1,512]{2,1,0:T(1,128)} %broadcast_select_fusion.refs_2_.refs_1_.refs_3_, ...), custom_call_target="tpu_custom_call" | custom-call | bytes 1024 | tf_op jit(solution)/shard_map/prepare_forward_1/pallas_call | solution.py:69
  34.9 5.6 %all-to-all-done.1 = bf16[16,32,256]{2,1,0:T(8,128)(2,1)S(1)} async-done(((bf16[16,32,256]{2,1,0:T(8,128)(2,1)}), bf16[16,32,256]{2,1,0:T(8,128)(2,1)S(1)}, u32[]{:S(2)}, u32[]{:S(2)}) %all-to-all-start.1) | async-done | bytes 262176 | tf_op jit(solution)/shard_map/all_to_all | solution.py:232
  40.5 1.5 %forward_1.1 = (bf16[512,256]{1,0:T(8,128)(2,1)}, bf16[512,256]{1,0:T(8,128)(2,1)}, f32[512,256]{1,0:T(8,128)}, bf16[512,256]{1,0:T(8,128)(2,1)}) custom-call(bf16[512,256]{1,0:T(8,128)(2,1)S(1)} %bitcast.28, bf16[512,256]{1,0:T(8,128)(2,1)S(1)} %get-tuple-element.90.refs_1_, f32[512,128]{1,0:T(8,128)S(1)} %get-tuple-element.91.refs_2_, ...), custom_call_target="tpu_custom_call" | custom-call | bytes 3145728 | tf_op jit(solution)/shard_map/forward_1/pallas_call | solution.py:69
  42.1 5.8 %all-to-all-start.2 = ((bf16[16,32,256]{2,1,0:T(8,128)(2,1)}), bf16[16,32,256]{2,1,0:T(8,128)(2,1)S(1)}, u32[]{:S(2)}, u32[]{:S(2)}) async-start(bf16[16,32,256]{2,1,0:T(8,128)(2,1)} %bitcast.38), calls=%async_computation.2 | async-start | bytes 524288 | tf_op jit(solution)/shard_map/all_to_all | solution.py:232
  47.9 1.6 %prepare_turn.1 = (bf16[512,512]{1,0:T(8,128)(2,1)S(1)}, bf16[512,512]{1,0:T(8,128)(2,1)S(1)}, f32[512,128]{1,0:T(8,128)S(1)}, bf16[512,128]{1,0:T(8,128)(2,1)S(1)}) custom-call(bf16[1,3,4,128,128]{4,3,2,1,0:T(8,128)(2,1)} %refs_1_.13, f32[3,1,512]{2,1,0:T(1,128)} %broadcast_select_fusion.refs_2_.refs_1_.refs_3_, bf16[1,512,128]{2,1,0:T(8,128)(2,1)} %refs_6_.1, ...), custom_call_target="tpu_custom_call" | custom-call | bytes 1024 | tf_op jit(solution)/shard_map/prepare_turn/pallas_call | solution.py:69
  49.5 5.2 %all-to-all-done.2 = bf16[16,32,256]{2,1,0:T(8,128)(2,1)S(1)} async-done(((bf16[16,32,256]{2,1,0:T(8,128)(2,1)}), bf16[16,32,256]{2,1,0:T(8,128)(2,1)S(1)}, u32[]{:S(2)}, u32[]{:S(2)}) %all-to-all-start.2) | async-done | bytes 262176 | tf_op jit(solution)/shard_map/all_to_all | solution.py:232
  54.7 1.5 %turn.1 = (bf16[512,128]{1,0:T(8,128)(2,1)}, bf16[512,256]{1,0:T(8,128)(2,1)}, f32[512,256]{1,0:T(8,128)}, bf16[512,128]{1,0:T(8,128)(2,1)}) custom-call(bf16[512,256]{1,0:T(8,128)(2,1)S(1)} %bitcast.29, bf16[512,128]{1,0:T(8,128)(2,1)S(1)} %get-tuple-element.96.refs_1_, f32[512,128]{1,0:T(8,128)S(1)} %get-tuple-element.97.refs_2_, ...), custom_call_target="tpu_custom_call" | custom-call | bytes 2752512 | tf_op jit(solution)/shard_map/turn/pallas_call | solution.py:69
  56.1 5.4 %all-to-all-start.3 = ((bf16[16,32,128]{2,1,0:T(8,128)(2,1)}), bf16[16,32,128]{2,1,0:T(8,128)(2,1)S(1)}, u32[]{:S(2)}, u32[]{:S(2)}) async-start(bf16[16,32,128]{2,1,0:T(8,128)(2,1)} %bitcast.44), calls=%async_computation.3 | async-start | bytes 262144 | tf_op jit(solution)/shard_map/all_to_all | solution.py:232
  61.5 2.0 %window_0_1.1 = (bf16[512,512]{1,0:T(8,128)(2,1)S(1)}, bf16[512,512]{1,0:T(8,128)(2,1)S(1)}, f32[512,128]{1,0:T(8,128)S(1)}, bf16[512,128]{1,0:T(8,128)(2,1)S(1)}) custom-call(bf16[1,3,4,128,128]{4,3,2,1,0:T(8,128)(2,1)} %refs_0_.19, bf16[1,3,4,128,128]{4,3,2,1,0:T(8,128)(2,1)} %refs_1_.13, f32[3,1,512]{2,1,0:T(1,128)} %broadcast_select_fusion.refs_2_.refs_1_.refs_3_, ...), custom_call_target="tpu_custom_call" | custom-call | bytes 1024 | tf_op jit(solution)/shard_map/window_0_1/pallas_call | solution.py:69
  63.5 4.4 %all-to-all-done.3 = bf16[16,32,128]{2,1,0:T(8,128)(2,1)S(1)} async-done(((bf16[16,32,128]{2,1,0:T(8,128)(2,1)}), bf16[16,32,128]{2,1,0:T(8,128)(2,1)S(1)}, u32[]{:S(2)}, u32[]{:S(2)}) %all-to-all-start.3) | async-done | bytes 131104 | tf_op jit(solution)/shard_map/all_to_all | solution.py:232
  69.3 5.1 %all-to-all-start.4 = ((bf16[16,32,128]{2,1,0:T(8,128)(2,1)}), bf16[16,32,128]{2,1,0:T(8,128)(2,1)S(1)}, u32[]{:S(2)}, u32[]{:S(2)}) async-start(bf16[16,32,128]{2,1,0:T(8,128)(2,1)} %bitcast.41), calls=%async_computation.4 | async-start | bytes 262144 | tf_op jit(solution)/shard_map/all_to_all | solution.py:232
  74.4 2.0 %window_0_0.1 = (bf16[512,512]{1,0:T(8,128)(2,1)S(1)}, bf16[512,512]{1,0:T(8,128)(2,1)S(1)}, f32[512,128]{1,0:T(8,128)S(1)}, f32[512,128]{1,0:T(8,128)S(1)}) custom-call(bf16[1,3,4,128,128]{4,3,2,1,0:T(8,128)(2,1)} %refs_0_.19, bf16[1,3,4,128,128]{4,3,2,1,0:T(8,128)(2,1)} %refs_1_.13, f32[3,1,512]{2,1,0:T(1,128)} %broadcast_select_fusion.refs_2_.refs_1_.refs_3_, ...), custom_call_target="tpu_custom_call" | custom-call | bytes 1024 | tf_op jit(solution)/shard_map/window_0_0/pallas_call | solution.py:69
  76.4 4.4 %all-to-all-done.4 = bf16[16,32,128]{2,1,0:T(8,128)(2,1)S(1)} async-done(((bf16[16,32,128]{2,1,0:T(8,128)(2,1)}), bf16[16,32,128]{2,1,0:T(8,128)(2,1)S(1)}, u32[]{:S(2)}, u32[]{:S(2)}) %all-to-all-start.4) | async-done | bytes 131104 | tf_op jit(solution)/shard_map/all_to_all | solution.py:232
  82.3 5.2 %all-to-all-start.5 = ((bf16[16,32,128]{2,1,0:T(8,128)(2,1)}), bf16[16,32,128]{2,1,0:T(8,128)(2,1)S(1)}, u32[]{:S(2)}, u32[]{:S(2)}) async-start(bf16[16,32,128]{2,1,0:T(8,128)(2,1)} %bitcast.43), calls=%async_computation.5 | async-start | bytes 262144 | tf_op jit(solution)/shard_map/all_to_all | solution.py:232
  88.1 2.0 %window_emit.1 = (bf16[512,512]{1,0:T(8,128)(2,1)S(1)}, f32[512,128]{1,0:T(8,128)S(1)}, bf16[512,512]{1,0:T(8,128)(2,1)S(1)}, f32[512,128]{1,0:T(8,128)S(1)}, bf16[512,128]{1,0:T(8,128)(2,1)S(1)}) custom-call(bf16[1,3,4,128,128]{4,3,2,1,0:T(8,128)(2,1)} %refs_0_.19, f32[512,128]{1,0:T(8,128)} %get-tuple-element.116.refs_1_.refs_5_, ...), custom_call_target="tpu_custom_call" | custom-call | bytes 1024 | tf_op jit(solution)/shard_map/window_emit/pallas_call | solution.py:69
  90.2 3.7 %all-to-all-done.5 = bf16[16,32,128]{2,1,0:T(8,128)(2,1)S(1)} async-done(((bf16[16,32,128]{2,1,0:T(8,128)(2,1)}), bf16[16,32,128]{2,1,0:T(8,128)(2,1)S(1)}, u32[]{:S(2)}, u32[]{:S(2)}) %all-to-all-start.5) | async-done | bytes 131104 | tf_op jit(solution)/shard_map/all_to_all | solution.py:232
  95.8 1.9 %collective-permute-done.refs_0_ = bf16[512,128]{1,0:T(8,128)(2,1)S(1)} collective-permute-done((bf16[512,128]{1,0:T(8,128)(2,1)S(1)}, bf16[512,128]{1,0:T(8,128)(2,1)S(1)}, u32[]{:S(2)}, u32[]{:S(2)}) %collective-permute-start) | collective-permute-done | bytes 131104 | tf_op jit(solution)/shard_map/ppermute | solution.py:519
  98.8 5.1 %all-to-all-start.6 = ((bf16[16,32,128]{2,1,0:T(8,128)(2,1)}), bf16[16,32,128]{2,1,0:T(8,128)(2,1)S(1)}, u32[]{:S(2)}, u32[]{:S(2)}) async-start(bf16[16,32,128]{2,1,0:T(8,128)(2,1)} %bitcast.42), calls=%async_computation.6 | async-start | bytes 262144 | tf_op jit(solution)/shard_map/all_to_all | solution.py:232
  104.5 3.9 %window_1_1.1 = (bf16[512,512]{1,0:T(8,128)(2,1)S(1)}, bf16[512,512]{1,0:T(8,128)(2,1)S(1)}, f32[512,128]{1,0:T(8,128)S(1)}, bf16[512,128]{1,0:T(8,128)(2,1)S(1)...) custom-call(bf16[1,3,4,128,128]{4,3,2,1,0:T(8,128)(2,1)} %refs_0_.19, ...), custom_call_target="tpu_custom_call" | custom-call | bytes 1024 | tf_op jit(solution)/shard_map/window_1_1/pallas_call | solution.py:69
  108.4 1.8 %all-to-all-done.6 = bf16[16,32,128]{2,1,0:T(8,128)(2,1)S(1)} async-done(((bf16[16,32,128]{2,1,0:T(8,128)(2,1)}), bf16[16,32,128]{2,1,0:T(8,128)(2,1)S(1)}, u32[]{:S(2)}, u32[]{:S(2)}) %all-to-all-start.6) | async-done | bytes 131104 | tf_op jit(solution)/shard_map/all_to_all | solution.py:232
  111.7 5.4 %all-to-all-start.7 = ((bf16[16,32,128]{2,1,0:T(8,128)(2,1)}), bf16[16,32,128]{2,1,0:T(8,128)(2,1)S(1)}, u32[]{:S(2)}, u32[]{:S(2)}) async-start(bf16[16,32,128]{2,1,0:T(8,128)(2,1)} %bitcast.40), calls=%async_computation.7 | async-start | bytes 262144 | tf_op jit(solution)/shard_map/all_to_all | solution.py:232
  117.1 4.5 %window_1_0.1 = (bf16[512,512]{1,0:T(8,128)(2,1)S(1)}, bf16[512,512]{1,0:T(8,128)(2,1)S(1)}, f32[512,128]{1,0:T(8,128)S(1)}, f32[512,128]{1,0:T(8,128)S(1)}, f32...) custom-call(bf16[1,3,4,128,128]{4,3,2,1,0:T(8,128)(2,1)} %refs_0_.19, ...), custom_call_target="tpu_custom_call", output_to_operand_aliasing={{4}: (15, {}), {5}: (16, {})} | custom-call | bytes 1024 | tf_op jit(solution)/shard_map/window_1_0/pallas_call | solution.py:69
  121.6 1.9 %all-to-all-done.7 = bf16[16,32,128]{2,1,0:T(8,128)(2,1)S(1)} async-done(((bf16[16,32,128]{2,1,0:T(8,128)(2,1)}), bf16[16,32,128]{2,1,0:T(8,128)(2,1)S(1)}, u32[]{:S(2)}, u32[]{:S(2)}) %all-to-all-start.7) | async-done | bytes 131104 | tf_op jit(solution)/shard_map/all_to_all | solution.py:232
  124.9 5.4 %all-to-all-start.8 = ((bf16[16,32,128]{2,1,0:T(8,128)(2,1)}), bf16[16,32,128]{2,1,0:T(8,128)(2,1)S(1)}, u32[]{:S(2)}, u32[]{:S(2)}) async-start(bf16[16,32,128]{2,1,0:T(8,128)(2,1)} %bitcast.39), calls=%async_computation.8 | async-start | bytes 262144 | tf_op jit(solution)/shard_map/all_to_all | solution.py:232
  130.3 3.9 %window_close.1 = (bf16[512,512]{1,0:T(8,128)(2,1)S(1)}, f32[512,128]{1,0:T(8,128)S(1)}, bf16[512,128]{1,0:T(8,128)(2,1)S(1)}, bf16[512,256]{1,0:T(8,128)(2,1)S(...) custom-call(bf16[1,3,4,128,128]{4,3,2,1,0:T(8,128)(2,1)} %refs_0_.19, ...), custom_call_target="tpu_custom_call", output_to_operand_aliasing={{4}: (14, {}), {5}: (15, {}), {6}: (16, {})} | custom-call | bytes 1024 | tf_op jit(solution)/shard_map/window_close/pallas_call | solution.py:69
  134.2 2.5 %all-to-all-done.8 = bf16[16,32,128]{2,1,0:T(8,128)(2,1)S(1)} async-done(((bf16[16,32,128]{2,1,0:T(8,128)(2,1)}), bf16[16,32,128]{2,1,0:T(8,128)(2,1)S(1)}, u32[]{:S(2)}, u32[]{:S(2)}) %all-to-all-start.8) | async-done | bytes 131104 | tf_op jit(solution)/shard_map/all_to_all | solution.py:232
  (17 shorter events, 12.1 us)
Async XLA Ops:
  2.9 17.2 %copy-start.1 = (f32[1,3,512]{2,0,1:T(1,128)S(1)}, f32[1,3,512]{2,0,1:T(1,128)}, u32[]{:S(2)}) copy-start(f32[1,3,512]{2,0,1:T(1,128)} %param.12) | copy-start | bytes 18436
  2.9 23.6 %all-to-all-start = ((bf16[16,32,256]{2,1,0:T(8,128)(2,1)}), bf16[16,32,256]{2,1,0:T(8,128)(2,1)S(1)}, u32[]{:S(2)}, u32[]{:S(2)}) async-start(bf16[16,32,256]{2,1,0:T(8,128)(2,1)} %bitcast.36), calls=%async_computation | async-start | bytes 524288 | tf_op jit(solution)/shard_map/all_to_all | solution.py:232
  28.0 12.5 %all-to-all-start.1 = ((bf16[16,32,256]{2,1,0:T(8,128)(2,1)}), bf16[16,32,256]{2,1,0:T(8,128)(2,1)S(1)}, u32[]{:S(2)}, u32[]{:S(2)}) async-start(bf16[16,32,256]{2,1,0:T(8,128)(2,1)} %bitcast.37), calls=%async_computation.1 | async-start | bytes 524288 | tf_op jit(solution)/shard_map/all_to_all | solution.py:232
  42.1 12.6 %all-to-all-start.2 = ((bf16[16,32,256]{2,1,0:T(8,128)(2,1)}), bf16[16,32,256]{2,1,0:T(8,128)(2,1)S(1)}, u32[]{:S(2)}, u32[]{:S(2)}) async-start(bf16[16,32,256]{2,1,0:T(8,128)(2,1)} %bitcast.38), calls=%async_computation.2 | async-start | bytes 524288 | tf_op jit(solution)/shard_map/all_to_all | solution.py:232
  56.1 11.8 %all-to-all-start.3 = ((bf16[16,32,128]{2,1,0:T(8,128)(2,1)}), bf16[16,32,128]{2,1,0:T(8,128)(2,1)S(1)}, u32[]{:S(2)}, u32[]{:S(2)}) async-start(bf16[16,32,128]{2,1,0:T(8,128)(2,1)} %bitcast.44), calls=%async_computation.3 | async-start | bytes 262144 | tf_op jit(solution)/shard_map/all_to_all | solution.py:232
  69.3 11.5 %all-to-all-start.4 = ((bf16[16,32,128]{2,1,0:T(8,128)(2,1)}), bf16[16,32,128]{2,1,0:T(8,128)(2,1)S(1)}, u32[]{:S(2)}, u32[]{:S(2)}) async-start(bf16[16,32,128]{2,1,0:T(8,128)(2,1)} %bitcast.41), calls=%async_computation.4 | async-start | bytes 262144 | tf_op jit(solution)/shard_map/all_to_all | solution.py:232
  82.3 5.2 %copy-start = (bf16[1,512,128]{2,1,0:T(8,128)(2,1)S(1)}, bf16[1,512,128]{2,1,0:T(8,128)(2,1)}, u32[]{:S(2)}) copy-start(bf16[1,512,128]{2,1,0:T(8,128)(2,1)} %param.9) | copy-start | bytes 393220
  82.3 11.6 %all-to-all-start.5 = ((bf16[16,32,128]{2,1,0:T(8,128)(2,1)}), bf16[16,32,128]{2,1,0:T(8,128)(2,1)S(1)}, u32[]{:S(2)}, u32[]{:S(2)}) async-start(bf16[16,32,128]{2,1,0:T(8,128)(2,1)} %bitcast.43), calls=%async_computation.5 | async-start | bytes 262144 | tf_op jit(solution)/shard_map/all_to_all | solution.py:232
  94.5 3.2 %collective-permute-start = (bf16[512,128]{1,0:T(8,128)(2,1)S(1)}, bf16[512,128]{1,0:T(8,128)(2,1)S(1)}, u32[]{:S(2)}, u32[]{:S(2)}) collective-permute-start(bf16[512,128]{1,0:T(8,128)(2,1)S(1)} %get-tuple-element.122), channel_id=1, source_target_pairs={{16,0},{32,16},{48,32},{64,48},{80,64},{96,80},{112,96},{128,112},... | collective-permute-start | bytes 393224 | tf_op jit(solution)/shard_map/ppermute | solution.py:519
  98.8 11.5 %all-to-all-start.6 = ((bf16[16,32,128]{2,1,0:T(8,128)(2,1)}), bf16[16,32,128]{2,1,0:T(8,128)(2,1)S(1)}, u32[]{:S(2)}, u32[]{:S(2)}) async-start(bf16[16,32,128]{2,1,0:T(8,128)(2,1)} %bitcast.42), calls=%async_computation.6 | async-start | bytes 262144 | tf_op jit(solution)/shard_map/all_to_all | solution.py:232
  111.7 11.8 %all-to-all-start.7 = ((bf16[16,32,128]{2,1,0:T(8,128)(2,1)}), bf16[16,32,128]{2,1,0:T(8,128)(2,1)S(1)}, u32[]{:S(2)}, u32[]{:S(2)}) async-start(bf16[16,32,128]{2,1,0:T(8,128)(2,1)} %bitcast.40), calls=%async_computation.7 | async-start | bytes 262144 | tf_op jit(solution)/shard_map/all_to_all | solution.py:232
  124.9 11.8 %all-to-all-start.8 = ((bf16[16,32,128]{2,1,0:T(8,128)(2,1)}), bf16[16,32,128]{2,1,0:T(8,128)(2,1)S(1)}, u32[]{:S(2)}, u32[]{:S(2)}) async-start(bf16[16,32,128]{2,1,0:T(8,128)(2,1)} %bitcast.39), calls=%async_computation.8 | async-start | bytes 262144 | tf_op jit(solution)/shard_map/all_to_all | solution.py:232

commit v2 on v1

--- a/solution.py
+++ b/solution.py
@@ -35,7 +35,7 @@
         sinks, refs = refs[: len(shapes)], refs[len(shapes) :]
         loaded, refs = refs[: len(loads)], refs[len(loads) :]
         staged, refs = refs[: len(stores)], refs[len(stores) :]
-        in_sems, out_sems = refs
+        in_sems, out_sems, half_sems = refs
         copies = [
             pltpu.make_async_copy(at(source, place), buffer, in_sems.at[number])
             for number, (source, place, buffer) in enumerate(zip(sources, places, loaded))
@@ -44,13 +44,30 @@
             copy.start()
         pending = []
 
-        def emit(number, value, ref=None):
+        def emit(number, value=None, ref=None):
             if ref is None:
                 ref = staged[number]
+            if value is not None:
                 ref[...] = value
             copy = pltpu.make_async_copy(ref, at(sinks[number], targets[number]), out_sems.at[number])
             copy.start()
             pending.append(copy)
+
+        def emit_product(number, left, right, chunks):
+            size = staged[number].shape[0] // chunks
+            for chunk in range(chunks):
+                rows = slice(chunk * size, (chunk + 1) * size)
+                staged[number][rows, :] = dot(left[rows, :], right[...]).astype(BF16)
+                if (chunk + 1) * 2 % chunks == 0:
+                    part = (chunk + 1) * 2 // chunks - 1
+                    half = slice(part * size * chunks // 2, (part + 1) * size * chunks // 2)
+                    copy = pltpu.make_async_copy(
+                        staged[number].at[half, :], sinks[number].at[half, :], half_sems.at[part]
+                    )
+                    copy.start()
+                    pending.append(copy)
+
+        emit.product, emit.staged = emit_product, staged
 
         waited = set()
 
@@ -76,6 +93,7 @@
             *stores,
             pltpu.SemaphoreType.DMA((max(1, len(loads)),)),
             pltpu.SemaphoreType.DMA((max(1, len(stores)),)),
+            pltpu.SemaphoreType.DMA((2,)),
         ],
         input_output_aliases=alias,
         name=name,
@@ -275,7 +293,7 @@
             ],
             axis=0,
         )
-        emit(0, dot(order, natural).astype(BF16))
+        emit.product(0, order, natural, blocks)
 
     (send,) = call(
         open_chain, "open", h_in=[first_of(0), (section_inputs, (0,))], h_out=[wide], chain=True
@@ -311,11 +329,18 @@
         def forward(emit, load, views, results):
             received, hidden, gate_now, second_now, first_now = views
             emit(1, None, received)
-            mixed = dot(second_now[...], received[...])
-            emit(2, mixed)
-            fresh = (hidden[...].astype(F32) + both(gate_now[...]) * branch_of(mixed)).astype(BF16)
-            emit(3, fresh)
-            emit(0, dot(first_now[...], fresh).astype(BF16))
+            mixed, fresh = emit.staged[2], emit.staged[3]
+            for block in range(blocks):
+                span = slice(block * size, (block + 1) * size)
+                mixed_now = dot(second_now[span, :], received[...])
+                mixed[span, :] = mixed_now
+                gates = both(gate_now[span, :])
+                fresh[span, :] = (
+                    hidden[span, :].astype(F32) + gates * branch_of(mixed_now)
+                ).astype(BF16)
+            emit(2)
+            emit(3)
+            emit.product(0, first_now, fresh, blocks)
 
         send, wire, mixed, fresh = call(
             forward,
@@ -347,12 +372,16 @@
     def turn(emit, load, views, results):
         received, arriving, gate_now, second_now, back_now = views
         emit(1, None, received)
-        mixed = dot(second_now[...], received[...])
-        emit(2, mixed)
-        slope = slope_of(mixed[:, :tokens], gate_now[...])
-        scaled = (arriving[...].astype(F32) * slope).astype(BF16)
-        emit(3, scaled)
-        emit(0, dot(back_now[...], scaled).astype(BF16))
+        mixed, scaled = emit.staged[2], emit.staged[3]
+        for block in range(blocks):
+            span = slice(block * size, (block + 1) * size)
+            mixed_now = dot(second_now[span, :], received[...])
+            mixed[span, :] = mixed_now
+            slope = slope_of(mixed_now[:, :tokens], gate_now[span, :])
+            scaled[span, :] = (arriving[span, :].astype(F32) * slope).astype(BF16)
+        emit(2)
+        emit(3)
+        emit.product(0, back_now, scaled, blocks)
 
     send, wire, mixed, scaled = call(
         turn,
@@ -457,11 +486,15 @@
         def backward(emit, load, views, results):
             received, grad, slope, first_now, second_now = views
             emit(1, None, received)
-            grad_now = grad[...].astype(F32) + dot(first_now[...], received[...])
-            emit(3, grad_now)
-            scaled = (grad_now * slope[...]).astype(BF16)
-            emit(2, scaled)
-            emit(0, dot(second_now[...], scaled).astype(BF16))
+            scaled, grad_out = emit.staged[2], emit.staged[3]
+            for block in range(blocks):
+                span = slice(block * size, (block + 1) * size)
+                grad_now = grad[span, :].astype(F32) + dot(first_now[span, :], received[...])
+                grad_out[span, :] = grad_now
+                scaled[span, :] = (grad_now * slope[span, :]).astype(BF16)
+            emit(3)
+            emit(2)
+            emit.product(0, second_now, scaled, blocks)
 
         send, returned, scaled, grad = call(
             backward,
@@ -505,34 +538,29 @@
 
     def emit_grad(emit, load, views, results):
         received, grad, first_now = views[:3]
-        emit(0, None, received)
         results[0][...] = (grad[...] + dot(first_now[...], received[...])).astype(BF16)
 
-    emitted, returns[0][0] = call(
-        emit_grad,
-        "emit",
-        v_in=[exchange(send, parts), grad, first_now, loss],
-        v_out=[slim],
-        h_out=[slim],
-        chain=True,
+    returned = exchange(send, parts)
+    (emitted,) = call(
+        emit_grad, "emit", v_in=[returned, grad, first_now, loss], v_out=[slim], chain=True
     )
     shifted = lax.ppermute(
         emitted, "section", [(source, source - 1) for source in range(1, sections)]
     )
 
     def again(emit, load, views, results):
-        shifted, loss, slope, second_now = views
+        shifted, loss, slope, second_now, returned = views
+        emit(3, None, returned)
         grad_now = shifted[...].astype(F32) + loss[...].astype(F32)
         emit(2, grad_now.astype(BF16))
-        scaled = (grad_now * slope[...]).astype(BF16)
-        emit(1, scaled)
-        emit(0, dot(second_now[...], scaled).astype(BF16))
-
-    send, scaleds[1][last], grads[1][last] = call(
+        emit(1, (grad_now * slope[...]).astype(BF16))
+        emit.product(0, second_now, emit.staged[1], blocks)
+
+    send, scaleds[1][last], grads[1][last], returns[0][0] = call(
         again,
         "again",
-        v_in=[shifted, loss, slope, second_now],
-        h_out=[slim, slim, slim],
+        v_in=[shifted, loss, slope, second_now, returned],
+        h_out=[slim, slim, slim, slim],
         chain=True,
     )
     started = scaleds[1][last]
@@ -550,32 +578,42 @@
     def prepare_close(emit, load, views, results):
         put_rows(results[0], first_back(sizes, load(0)))
         results[1][...] = load(1)[...]
-        results[2][...] = load(2)[...]
+        order = first_rows(sizes, 1)
+        results[2][...] = order
         inputs = load(3)
-        results[3][...] = jnp.concatenate([inputs[0], inputs[1]], axis=1)
+        results[3][...] = inputs[1]
+        natural = dot(order, load(2)[...]).astype(BF16)
+        for block in range(blocks):
+            span = slice(block * size, (block + 1) * size)
+            results[4][span, :] = dot_t(natural[span], inputs[0, span, :])
 
     task = (
         prepare_close,
         [first_of(0), grads[1][0], returns[0][0], (section_inputs, (0,))],
-        [square, slim_f32, slim, wide],
+        [square, slim_f32, square, slim, shape(size, F32)],
         [],
         [],
     )
-    (first_now, grad, earlier, hidden), (gate_out,), (second_out,), (first_out,) = merged(
+    (first_now, grad, order, hidden, sums), (gate_out,), (second_out,), (first_out,) = merged(
         "window_close",
         [task, gate_sums(0, gate_out), second_sums(0, second_out), first_sums(1, first_out)],
         [started],
     )
 
     def close(emit, load, views, results):
-        received, grad, first_now, earlier, hidden = views
+        received, grad, first_now, order, hidden, sums = views
+        factor_out = emit.staged[1]
+        natural = dot(order[...], received[...]).astype(BF16)
         emit(0, (grad[...] + dot(first_now[...], received[...])).astype(BF16))
-        emit(1, first_sum(earlier[...], received[...], hidden[...]))
+        for block in range(blocks):
+            span = slice(block * size, (block + 1) * size)
+            factor_out[block] = (sums[span, :] + dot_t(natural[span], hidden[span, :])).astype(BF16)
+        emit(1)
 
     emitted, first_out = call(
         close,
         "close",
-        v_in=[exchange(send, parts), grad, first_now, earlier, hidden],
+        v_in=[exchange(send, parts), grad, first_now, order, hidden, sums],
         h_out=[slim, (factor_shape, (0, 0))],
         into=[(1, first_out)],
         chain=True,

time: 139 us -> 138 us (level)
  transfers between devices with their start and end apart: 10 -> 10, of which waited for: 10 -> 10; matrix products, arithmetic and copies ran while one was open for 1% -> 1% of each run, Pallas kernels for 17% -> 18%
where the time goes in v2:
time: 138 us; the launch traced here: 137 us
  starting transfers between devices  60.4 us (44%)
  Pallas kernels  37.9 us (27%)
  waiting for transfers between devices  35 us (25%)
  between operations  1.65 us (1%)
    all_to_all x9, starting transfers between devices, exchange(): lax.all_to_all(shaped, 'tensor', 0, 0, tiled=True).reshape(rows, columns)  59.1 us
    pallas_call x20, Pallas kernels, call(): pl.pallas_call(kernel, out_shape=[*v_out, *(pltpu.HBM(a.shape, a.dtype) f...  37.9 us
    all_to_all x9, waiting for transfers between devices, exchange(): lax.all_to_all(shaped, 'tensor', 0, 0, tiled=True).reshape(rows, columns)  33 us
  transfers between devices with their start and end apart: 10, of which 10 were waited for; matrix products, arithmetic and copies ran while one was open for 1% of the time, Pallas kernels for 18%

profile of v2, /device:TPU:2, one launch (start us, length us, event | category | flops | bytes accessed | tf_op | source)
XLA Modules:
  0.0 137.0 jit_solution(6581924134451200103)
XLA Ops:
  0.6 2.2 %open.1 = bf16[512,256]{1,0:T(8,128)(2,1)} custom-call(bf16[1,3,4,128,128]{4,3,2,1,0:T(8,128)(2,1)} %refs_0_.19, bf16[1,2,512,128]{3,2,1,0:T(8,128)(2,1)} %refs_3_.3), custom_call_target="tpu_custom_call" | custom-call | bytes 917504 | tf_op jit(solution)/shard_map/open/pallas_call | solution.py:86
  2.8 16.5 %all-to-all-start = ((bf16[16,32,256]{2,1,0:T(8,128)(2,1)}), bf16[16,32,256]{2,1,0:T(8,128)(2,1)S(1)}, u32[]{:S(2)}, u32[]{:S(2)}) async-start(bf16[16,32,256]{2,1,0:T(8,128)(2,1)} %bitcast.37), calls=%async_computation | async-start | bytes 524288 | tf_op jit(solution)/shard_map/all_to_all | solution.py:250
  20.7 1.8 %prepare_forward_0.1 = (bf16[512,512]{1,0:T(8,128)(2,1)S(1)}, bf16[512,512]{1,0:T(8,128)(2,1)S(1)}, f32[512,128]{1,0:T(8,128)S(1)}, bf16[512,256]{1,0:T(8,128)(2,1)S(1)}) custom-call(bf16[1,3,4,128,128]{4,3,2,1,0:T(8,128)(2,1)} %refs_1_.13, bf16[1,3,4,128,128]{4,3,2,1,0:T(8,128)(2,1)} %refs_0_.19, f32[3,1,512]{2,1,0:T(1,128)} %broadcast_select_fusion.refs_2_.refs_1_.refs_3_, ...), custom_call_target="tpu_custom_call" | custom-call | bytes 1024 | tf_op jit(solution)/shard_map/prepare_forward_0/pallas_call | solution.py:86
  22.5 3.9 %all-to-all-done = bf16[16,32,256]{2,1,0:T(8,128)(2,1)S(1)} async-done(((bf16[16,32,256]{2,1,0:T(8,128)(2,1)}), bf16[16,32,256]{2,1,0:T(8,128)(2,1)S(1)}, u32[]{:S(2)}, u32[]{:S(2)}) %all-to-all-start) | async-done | bytes 262176 | tf_op jit(solution)/shard_map/all_to_all | solution.py:250
  26.4 1.4 %forward_0.1 = (bf16[512,256]{1,0:T(8,128)(2,1)}, bf16[512,256]{1,0:T(8,128)(2,1)}, f32[512,256]{1,0:T(8,128)}, bf16[512,256]{1,0:T(8,128)(2,1)}) custom-call(bf16[512,256]{1,0:T(8,128)(2,1)S(1)} %bitcast.29, bf16[512,256]{1,0:T(8,128)(2,1)S(1)} %get-tuple-element.84.refs_1_, f32[512,128]{1,0:T(8,128)S(1)} %get-tuple-element.85.refs_2_, ...), custom_call_target="tpu_custom_call" | custom-call | bytes 3145728 | tf_op jit(solution)/shard_map/forward_0/pallas_call | solution.py:86
  27.8 5.3 %all-to-all-start.1 = ((bf16[16,32,256]{2,1,0:T(8,128)(2,1)}), bf16[16,32,256]{2,1,0:T(8,128)(2,1)S(1)}, u32[]{:S(2)}, u32[]{:S(2)}) async-start(bf16[16,32,256]{2,1,0:T(8,128)(2,1)} %bitcast.38), calls=%async_computation.1 | async-start | bytes 524288 | tf_op jit(solution)/shard_map/all_to_all | solution.py:250
  33.2 1.8 %prepare_forward_1.1 = (bf16[512,512]{1,0:T(8,128)(2,1)S(1)}, bf16[512,512]{1,0:T(8,128)(2,1)S(1)}, f32[512,128]{1,0:T(8,128)S(1)}, bf16[512,256]{1,0:T(8,128)(2,1)S(1)}) custom-call(bf16[1,3,4,128,128]{4,3,2,1,0:T(8,128)(2,1)} %refs_1_.13, bf16[1,3,4,128,128]{4,3,2,1,0:T(8,128)(2,1)} %refs_0_.19, f32[3,1,512]{2,1,0:T(1,128)} %broadcast_select_fusion.refs_2_.refs_1_.refs_3_, ...), custom_call_target="tpu_custom_call" | custom-call | bytes 1024 | tf_op jit(solution)/shard_map/prepare_forward_1/pallas_call | solution.py:86
  34.9 5.8 %all-to-all-done.1 = bf16[16,32,256]{2,1,0:T(8,128)(2,1)S(1)} async-done(((bf16[16,32,256]{2,1,0:T(8,128)(2,1)}), bf16[16,32,256]{2,1,0:T(8,128)(2,1)S(1)}, u32[]{:S(2)}, u32[]{:S(2)}) %all-to-all-start.1) | async-done | bytes 262176 | tf_op jit(solution)/shard_map/all_to_all | solution.py:250
  40.7 1.4 %forward_1.1 = (bf16[512,256]{1,0:T(8,128)(2,1)}, bf16[512,256]{1,0:T(8,128)(2,1)}, f32[512,256]{1,0:T(8,128)}, bf16[512,256]{1,0:T(8,128)(2,1)}) custom-call(bf16[512,256]{1,0:T(8,128)(2,1)S(1)} %bitcast.30, bf16[512,256]{1,0:T(8,128)(2,1)S(1)} %get-tuple-element.90.refs_1_, f32[512,128]{1,0:T(8,128)S(1)} %get-tuple-element.91.refs_2_, ...), custom_call_target="tpu_custom_call" | custom-call | bytes 3145728 | tf_op jit(solution)/shard_map/forward_1/pallas_call | solution.py:86
  42.1 5.7 %all-to-all-start.2 = ((bf16[16,32,256]{2,1,0:T(8,128)(2,1)}), bf16[16,32,256]{2,1,0:T(8,128)(2,1)S(1)}, u32[]{:S(2)}, u32[]{:S(2)}) async-start(bf16[16,32,256]{2,1,0:T(8,128)(2,1)} %bitcast.39), calls=%async_computation.2 | async-start | bytes 524288 | tf_op jit(solution)/shard_map/all_to_all | solution.py:250
  47.9 1.6 %prepare_turn.1 = (bf16[512,512]{1,0:T(8,128)(2,1)S(1)}, bf16[512,512]{1,0:T(8,128)(2,1)S(1)}, f32[512,128]{1,0:T(8,128)S(1)}, bf16[512,128]{1,0:T(8,128)(2,1)S(1)}) custom-call(bf16[1,3,4,128,128]{4,3,2,1,0:T(8,128)(2,1)} %refs_1_.13, f32[3,1,512]{2,1,0:T(1,128)} %broadcast_select_fusion.refs_2_.refs_1_.refs_3_, bf16[1,512,128]{2,1,0:T(8,128)(2,1)} %refs_6_.1, ...), custom_call_target="tpu_custom_call" | custom-call | bytes 1024 | tf_op jit(solution)/shard_map/prepare_turn/pallas_call | solution.py:86
  49.5 5.2 %all-to-all-done.2 = bf16[16,32,256]{2,1,0:T(8,128)(2,1)S(1)} async-done(((bf16[16,32,256]{2,1,0:T(8,128)(2,1)}), bf16[16,32,256]{2,1,0:T(8,128)(2,1)S(1)}, u32[]{:S(2)}, u32[]{:S(2)}) %all-to-all-start.2) | async-done | bytes 262176 | tf_op jit(solution)/shard_map/all_to_all | solution.py:250
  54.7 1.3 turn.1
  56.0 5.4 %all-to-all-start.3 = ((bf16[16,32,128]{2,1,0:T(8,128)(2,1)}), bf16[16,32,128]{2,1,0:T(8,128)(2,1)S(1)}, u32[]{:S(2)}, u32[]{:S(2)}) async-start(bf16[16,32,128]{2,1,0:T(8,128)(2,1)} %bitcast.45), calls=%async_computation.3 | async-start | bytes 262144 | tf_op jit(solution)/shard_map/all_to_all | solution.py:250
  61.4 2.0 %window_0_1.1 = (bf16[512,512]{1,0:T(8,128)(2,1)S(1)}, bf16[512,512]{1,0:T(8,128)(2,1)S(1)}, f32[512,128]{1,0:T(8,128)S(1)}, bf16[512,128]{1,0:T(8,128)(2,1)S(1)}) custom-call(bf16[1,3,4,128,128]{4,3,2,1,0:T(8,128)(2,1)} %refs_0_.19, bf16[1,3,4,128,128]{4,3,2,1,0:T(8,128)(2,1)} %refs_1_.13, f32[3,1,512]{2,1,0:T(1,128)} %broadcast_select_fusion.refs_2_.refs_1_.refs_3_, ...), custom_call_target="tpu_custom_call" | custom-call | bytes 1024 | tf_op jit(solution)/shard_map/window_0_1/pallas_call | solution.py:86
  63.4 4.4 %all-to-all-done.3 = bf16[16,32,128]{2,1,0:T(8,128)(2,1)S(1)} async-done(((bf16[16,32,128]{2,1,0:T(8,128)(2,1)}), bf16[16,32,128]{2,1,0:T(8,128)(2,1)S(1)}, u32[]{:S(2)}, u32[]{:S(2)}) %all-to-all-start.3) | async-done | bytes 131104 | tf_op jit(solution)/shard_map/all_to_all | solution.py:250
  69.0 5.1 %all-to-all-start.4 = ((bf16[16,32,128]{2,1,0:T(8,128)(2,1)}), bf16[16,32,128]{2,1,0:T(8,128)(2,1)S(1)}, u32[]{:S(2)}, u32[]{:S(2)}) async-start(bf16[16,32,128]{2,1,0:T(8,128)(2,1)} %bitcast.42), calls=%async_computation.4 | async-start | bytes 262144 | tf_op jit(solution)/shard_map/all_to_all | solution.py:250
  74.1 2.0 %window_0_0.1 = (bf16[512,512]{1,0:T(8,128)(2,1)S(1)}, bf16[512,512]{1,0:T(8,128)(2,1)S(1)}, f32[512,128]{1,0:T(8,128)S(1)}, f32[512,128]{1,0:T(8,128)S(1)}) custom-call(bf16[1,3,4,128,128]{4,3,2,1,0:T(8,128)(2,1)} %refs_0_.19, bf16[1,3,4,128,128]{4,3,2,1,0:T(8,128)(2,1)} %refs_1_.13, f32[3,1,512]{2,1,0:T(1,128)} %broadcast_select_fusion.refs_2_.refs_1_.refs_3_, ...), custom_call_target="tpu_custom_call" | custom-call | bytes 1024 | tf_op jit(solution)/shard_map/window_0_0/pallas_call | solution.py:86
  76.1 4.4 %all-to-all-done.4 = bf16[16,32,128]{2,1,0:T(8,128)(2,1)S(1)} async-done(((bf16[16,32,128]{2,1,0:T(8,128)(2,1)}), bf16[16,32,128]{2,1,0:T(8,128)(2,1)S(1)}, u32[]{:S(2)}, u32[]{:S(2)}) %all-to-all-start.4) | async-done | bytes 131104 | tf_op jit(solution)/shard_map/all_to_all | solution.py:250
  81.8 5.2 %all-to-all-start.5 = ((bf16[16,32,128]{2,1,0:T(8,128)(2,1)}), bf16[16,32,128]{2,1,0:T(8,128)(2,1)S(1)}, u32[]{:S(2)}, u32[]{:S(2)}) async-start(bf16[16,32,128]{2,1,0:T(8,128)(2,1)} %bitcast.44), calls=%async_computation.5 | async-start | bytes 262144 | tf_op jit(solution)/shard_map/all_to_all | solution.py:250
  87.6 2.0 %window_emit.1 = (bf16[512,512]{1,0:T(8,128)(2,1)S(1)}, f32[512,128]{1,0:T(8,128)S(1)}, bf16[512,512]{1,0:T(8,128)(2,1)S(1)}, f32[512,128]{1,0:T(8,128)S(1)}, bf16[512,128]{1,0:T(8,128)(2,1)S(1)}) custom-call(bf16[1,3,4,128,128]{4,3,2,1,0:T(8,128)(2,1)} %refs_0_.19, f32[512,128]{1,0:T(8,128)} %get-tuple-element.116.refs_1_.refs_5_, ...), custom_call_target="tpu_custom_call" | custom-call | bytes 1024 | tf_op jit(solution)/shard_map/window_emit/pallas_call | solution.py:86
  89.7 3.7 %all-to-all-done.5 = bf16[16,32,128]{2,1,0:T(8,128)(2,1)S(1)} async-done(((bf16[16,32,128]{2,1,0:T(8,128)(2,1)}), bf16[16,32,128]{2,1,0:T(8,128)(2,1)S(1)}, u32[]{:S(2)}, u32[]{:S(2)}) %all-to-all-start.5) | async-done | bytes 131104 | tf_op jit(solution)/shard_map/all_to_all | solution.py:250
  95.0 1.9 %collective-permute-done.refs_0_ = bf16[512,128]{1,0:T(8,128)(2,1)S(1)} collective-permute-done((bf16[512,128]{1,0:T(8,128)(2,1)S(1)}, bf16[512,128]{1,0:T(8,128)(2,1)S(1)}, u32[]{:S(2)}, u32[]{:S(2)}) %collective-permute-start) | collective-permute-done | bytes 131104 | tf_op jit(solution)/shard_map/ppermute | solution.py:547
  98.0 5.1 %all-to-all-start.6 = ((bf16[16,32,128]{2,1,0:T(8,128)(2,1)}), bf16[16,32,128]{2,1,0:T(8,128)(2,1)S(1)}, u32[]{:S(2)}, u32[]{:S(2)}) async-start(bf16[16,32,128]{2,1,0:T(8,128)(2,1)} %bitcast.43), calls=%async_computation.6 | async-start | bytes 262144 | tf_op jit(solution)/shard_map/all_to_all | solution.py:250
  103.7 3.9 %window_1_1.1 = (bf16[512,512]{1,0:T(8,128)(2,1)S(1)}, bf16[512,512]{1,0:T(8,128)(2,1)S(1)}, f32[512,128]{1,0:T(8,128)S(1)}, bf16[512,128]{1,0:T(8,128)(2,1)S(1)...) custom-call(bf16[1,3,4,128,128]{4,3,2,1,0:T(8,128)(2,1)} %refs_0_.19, ...), custom_call_target="tpu_custom_call" | custom-call | bytes 1024 | tf_op jit(solution)/shard_map/window_1_1/pallas_call | solution.py:86
  107.6 1.8 %all-to-all-done.6 = bf16[16,32,128]{2,1,0:T(8,128)(2,1)S(1)} async-done(((bf16[16,32,128]{2,1,0:T(8,128)(2,1)}), bf16[16,32,128]{2,1,0:T(8,128)(2,1)S(1)}, u32[]{:S(2)}, u32[]{:S(2)}) %all-to-all-start.6) | async-done | bytes 131104 | tf_op jit(solution)/shard_map/all_to_all | solution.py:250
  110.7 5.4 %all-to-all-start.7 = ((bf16[16,32,128]{2,1,0:T(8,128)(2,1)}), bf16[16,32,128]{2,1,0:T(8,128)(2,1)S(1)}, u32[]{:S(2)}, u32[]{:S(2)}) async-start(bf16[16,32,128]{2,1,0:T(8,128)(2,1)} %bitcast.41), calls=%async_computation.7 | async-start | bytes 262144 | tf_op jit(solution)/shard_map/all_to_all | solution.py:250
  116.1 4.5 %window_1_0.1 = (bf16[512,512]{1,0:T(8,128)(2,1)S(1)}, bf16[512,512]{1,0:T(8,128)(2,1)S(1)}, f32[512,128]{1,0:T(8,128)S(1)}, f32[512,128]{1,0:T(8,128)S(1)}, f32...) custom-call(bf16[1,3,4,128,128]{4,3,2,1,0:T(8,128)(2,1)} %refs_0_.19, ...), custom_call_target="tpu_custom_call", output_to_operand_aliasing={{4}: (15, {}), {5}: (16, {})} | custom-call | bytes 1024 | tf_op jit(solution)/shard_map/window_1_0/pallas_call | solution.py:86
  120.7 1.8 %all-to-all-done.7 = bf16[16,32,128]{2,1,0:T(8,128)(2,1)S(1)} async-done(((bf16[16,32,128]{2,1,0:T(8,128)(2,1)}), bf16[16,32,128]{2,1,0:T(8,128)(2,1)S(1)}, u32[]{:S(2)}, u32[]{:S(2)}) %all-to-all-start.7) | async-done | bytes 131104 | tf_op jit(solution)/shard_map/all_to_all | solution.py:250
  123.8 5.4 %all-to-all-start.8 = ((bf16[16,32,128]{2,1,0:T(8,128)(2,1)}), bf16[16,32,128]{2,1,0:T(8,128)(2,1)S(1)}, u32[]{:S(2)}, u32[]{:S(2)}) async-start(bf16[16,32,128]{2,1,0:T(8,128)(2,1)} %bitcast.40), calls=%async_computation.8 | async-start | bytes 262144 | tf_op jit(solution)/shard_map/all_to_all | solution.py:250
  129.2 4.4 %window_close.1 = (bf16[512,512]{1,0:T(8,128)(2,1)S(1)}, f32[512,128]{1,0:T(8,128)S(1)}, bf16[512,512]{1,0:T(8,128)(2,1)S(1)}, bf16[512,128]{1,0:T(8,128)(2,1)S(...) custom-call(bf16[1,3,4,128,128]{4,3,2,1,0:T(8,128)(2,1)} %refs_0_.19, ...), custom_call_target="tpu_custom_call", output_to_operand_aliasing={{5}: (14, {}), {6}: (15, {}), {7}: (16, {})} | custom-call | bytes 1024 | tf_op jit(solution)/shard_map/window_close/pallas_call | solution.py:86
  133.6 2.0 %all-to-all-done.8 = bf16[16,32,128]{2,1,0:T(8,128)(2,1)S(1)} async-done(((bf16[16,32,128]{2,1,0:T(8,128)(2,1)}), bf16[16,32,128]{2,1,0:T(8,128)(2,1)S(1)}, u32[]{:S(2)}, u32[]{:S(2)}) %all-to-all-start.8) | async-done | bytes 131104 | tf_op jit(solution)/shard_map/all_to_all | solution.py:250
  (17 shorter events, 11.0 us)
Async XLA Ops:
  2.8 17.2 %copy-start.1 = (f32[1,3,512]{2,0,1:T(1,128)S(1)}, f32[1,3,512]{2,0,1:T(1,128)}, u32[]{:S(2)}) copy-start(f32[1,3,512]{2,0,1:T(1,128)} %param.12) | copy-start | bytes 18436
  2.8 23.6 %all-to-all-start = ((bf16[16,32,256]{2,1,0:T(8,128)(2,1)}), bf16[16,32,256]{2,1,0:T(8,128)(2,1)S(1)}, u32[]{:S(2)}, u32[]{:S(2)}) async-start(bf16[16,32,256]{2,1,0:T(8,128)(2,1)} %bitcast.37), calls=%async_computation | async-start | bytes 524288 | tf_op jit(solution)/shard_map/all_to_all | solution.py:250
  27.8 12.9 %all-to-all-start.1 = ((bf16[16,32,256]{2,1,0:T(8,128)(2,1)}), bf16[16,32,256]{2,1,0:T(8,128)(2,1)S(1)}, u32[]{:S(2)}, u32[]{:S(2)}) async-start(bf16[16,32,256]{2,1,0:T(8,128)(2,1)} %bitcast.38), calls=%async_computation.1 | async-start | bytes 524288 | tf_op jit(solution)/shard_map/all_to_all | solution.py:250
  42.1 12.5 %all-to-all-start.2 = ((bf16[16,32,256]{2,1,0:T(8,128)(2,1)}), bf16[16,32,256]{2,1,0:T(8,128)(2,1)S(1)}, u32[]{:S(2)}, u32[]{:S(2)}) async-start(bf16[16,32,256]{2,1,0:T(8,128)(2,1)} %bitcast.39), calls=%async_computation.2 | async-start | bytes 524288 | tf_op jit(solution)/shard_map/all_to_all | solution.py:250
  56.0 11.8 %all-to-all-start.3 = ((bf16[16,32,128]{2,1,0:T(8,128)(2,1)}), bf16[16,32,128]{2,1,0:T(8,128)(2,1)S(1)}, u32[]{:S(2)}, u32[]{:S(2)}) async-start(bf16[16,32,128]{2,1,0:T(8,128)(2,1)} %bitcast.45), calls=%async_computation.3 | async-start | bytes 262144 | tf_op jit(solution)/shard_map/all_to_all | solution.py:250
  69.0 11.5 %all-to-all-start.4 = ((bf16[16,32,128]{2,1,0:T(8,128)(2,1)}), bf16[16,32,128]{2,1,0:T(8,128)(2,1)S(1)}, u32[]{:S(2)}, u32[]{:S(2)}) async-start(bf16[16,32,128]{2,1,0:T(8,128)(2,1)} %bitcast.42), calls=%async_computation.4 | async-start | bytes 262144 | tf_op jit(solution)/shard_map/all_to_all | solution.py:250
  81.8 5.2 %copy-start = (bf16[1,512,128]{2,1,0:T(8,128)(2,1)S(1)}, bf16[1,512,128]{2,1,0:T(8,128)(2,1)}, u32[]{:S(2)}) copy-start(bf16[1,512,128]{2,1,0:T(8,128)(2,1)} %param.9) | copy-start | bytes 393220
  81.8 11.6 %all-to-all-start.5 = ((bf16[16,32,128]{2,1,0:T(8,128)(2,1)}), bf16[16,32,128]{2,1,0:T(8,128)(2,1)S(1)}, u32[]{:S(2)}, u32[]{:S(2)}) async-start(bf16[16,32,128]{2,1,0:T(8,128)(2,1)} %bitcast.44), calls=%async_computation.5 | async-start | bytes 262144 | tf_op jit(solution)/shard_map/all_to_all | solution.py:250
  93.7 3.2 %collective-permute-start = (bf16[512,128]{1,0:T(8,128)(2,1)S(1)}, bf16[512,128]{1,0:T(8,128)(2,1)S(1)}, u32[]{:S(2)}, u32[]{:S(2)}) collective-permute-start(bf16[512,128]{1,0:T(8,128)(2,1)S(1)} %emit.1), channel_id=1, source_target_pairs={{16,0},{32,16},{48,32},{64,48},{80,64},{96,80},{112,96},{128,112},... | collective-permute-start | bytes 393224 | tf_op jit(solution)/shard_map/ppermute | solution.py:547
  98.0 11.5 %all-to-all-start.6 = ((bf16[16,32,128]{2,1,0:T(8,128)(2,1)}), bf16[16,32,128]{2,1,0:T(8,128)(2,1)S(1)}, u32[]{:S(2)}, u32[]{:S(2)}) async-start(bf16[16,32,128]{2,1,0:T(8,128)(2,1)} %bitcast.43), calls=%async_computation.6 | async-start | bytes 262144 | tf_op jit(solution)/shard_map/all_to_all | solution.py:250
  110.7 11.8 %all-to-all-start.7 = ((bf16[16,32,128]{2,1,0:T(8,128)(2,1)}), bf16[16,32,128]{2,1,0:T(8,128)(2,1)S(1)}, u32[]{:S(2)}, u32[]{:S(2)}) async-start(bf16[16,32,128]{2,1,0:T(8,128)(2,1)} %bitcast.41), calls=%async_computation.7 | async-start | bytes 262144 | tf_op jit(solution)/shard_map/all_to_all | solution.py:250
  123.8 11.8 %all-to-all-start.8 = ((bf16[16,32,128]{2,1,0:T(8,128)(2,1)}), bf16[16,32,128]{2,1,0:T(8,128)(2,1)S(1)}, u32[]{:S(2)}, u32[]{:S(2)}) async-start(bf16[16,32,128]{2,1,0:T(8,128)(2,1)} %bitcast.40), calls=%async_computation.8 | async-start | bytes 262144 | tf_op jit(solution)/shard_map/all_to_all | solution.py:250

commit v3 on v2

--- a/solution.py
+++ b/solution.py
@@ -270,7 +270,7 @@
         return jax.ShapeDtypeStruct((rows, columns), dtype)
 
     wide, slim, square = shape(2 * tokens), shape(tokens), shape(rows)
-    wide_f32, slim_f32 = shape(2 * tokens, F32), shape(tokens, F32)
+    slim_f32 = shape(tokens, F32)
     factor_shape = jax.ShapeDtypeStruct(factor_first.shape, BF16)
 
     def first_of(slot):
@@ -329,28 +329,30 @@
         def forward(emit, load, views, results):
             received, hidden, gate_now, second_now, first_now = views
             emit(1, None, received)
-            mixed, fresh = emit.staged[2], emit.staged[3]
+            mixed, fresh, mixed_later = emit.staged[2], emit.staged[3], emit.staged[4]
             for block in range(blocks):
                 span = slice(block * size, (block + 1) * size)
                 mixed_now = dot(second_now[span, :], received[...])
-                mixed[span, :] = mixed_now
+                mixed[span, :] = mixed_now[:, :tokens]
+                mixed_later[span, :] = mixed_now[:, tokens:]
                 gates = both(gate_now[span, :])
                 fresh[span, :] = (
                     hidden[span, :].astype(F32) + gates * branch_of(mixed_now)
                 ).astype(BF16)
             emit(2)
+            emit(4)
             emit(3)
             emit.product(0, first_now, fresh, blocks)
 
-        send, wire, mixed, fresh = call(
+        send, wire, mixed, fresh, mixed_later = call(
             forward,
             f"forward_{slot}",
             v_in=[exchange(send, parts), hidden, gate_now, second_now, first_now],
-            h_out=[wide, wide, wide_f32, wide],
+            h_out=[wide, wide, slim_f32, wide, slim_f32],
             chain=True,
         )
         wires.append(wire)
-        mixeds.append(mixed)
+        mixeds.append((mixed, mixed_later))
         hiddens.append(fresh)
         started = fresh
 
@@ -372,26 +374,28 @@
     def turn(emit, load, views, results):
         received, arriving, gate_now, second_now, back_now = views
         emit(1, None, received)
-        mixed, scaled = emit.staged[2], emit.staged[3]
+        mixed, scaled, mixed_later = emit.staged[2], emit.staged[3], emit.staged[4]
         for block in range(blocks):
             span = slice(block * size, (block + 1) * size)
             mixed_now = dot(second_now[span, :], received[...])
-            mixed[span, :] = mixed_now
+            mixed[span, :] = mixed_now[:, :tokens]
+            mixed_later[span, :] = mixed_now[:, tokens:]
             slope = slope_of(mixed_now[:, :tokens], gate_now[span, :])
             scaled[span, :] = (arriving[span, :].astype(F32) * slope).astype(BF16)
         emit(2)
+        emit(4)
         emit(3)
         emit.product(0, back_now, scaled, blocks)
 
-    send, wire, mixed, scaled = call(
+    send, wire, mixed, scaled, mixed_later = call(
         turn,
         "turn",
         v_in=[exchange(send, parts), arriving, gate_now, second_now, back_now],
-        h_out=[slim, wide, wide_f32, slim],
+        h_out=[slim, wide, slim_f32, slim, slim_f32],
         chain=True,
     )
     wires.append(wire)
-    mixeds.append(mixed)
+    mixeds.append((mixed, mixed_later))
     started = scaled
 
     scaleds = [[None] * slots, [None] * slots]
@@ -400,17 +404,32 @@
     scaleds[0][last], grads[0][last] = scaled, (arriving_grad, (0,))
     gate_shape = jax.ShapeDtypeStruct(gate.shape, F32)
 
+    gate_parts = [None] * slots
+
+    def gate_terms(load):
+        terms = load(1)[...].astype(F32) * branch_of(load(0)[...])
+        return jnp.sum(terms.T, axis=0, keepdims=True)
+
+    def gate_first(slot):
+        def body(emit, load, views, results):
+            emit(0, gate_terms(load))
+
+        return (
+            body,
+            [mixeds[slot][0], grads[0][slot]],
+            [],
+            [jax.ShapeDtypeStruct((1, rows), F32)],
+            [],
+        )
+
     def gate_sums(slot, filled):
         def body(emit, load, views, results):
-            branch = branch_of(load(0)[...])
-            terms = load(1)[...].astype(F32) * branch[:, :tokens]
-            terms += load(2)[...].astype(F32) * branch[:, tokens:]
-            sums = jnp.sum(terms.T, axis=0, keepdims=True)
-            emit(0, jnp.where(load(3)[...] > 0, sums, 0.0))
+            sums = load(3)[...] + gate_terms(load)
+            emit(0, jnp.where(load(2)[...] > 0, sums, 0.0))
 
         return (
             body,
-            [mixeds[slot], grads[0][slot], grads[1][slot], (alive, (slot,))],
+            [mixeds[slot][1], grads[1][slot], (alive, (slot,)), gate_parts[slot]],
             [],
             [(gate_shape, (slot,))],
             [] if filled is None else [(0, filled)],
@@ -457,14 +476,13 @@
         )
 
     def step(moment, slot, send, started, tasks=()):
-        columns = slice(moment * tokens, (moment + 1) * tokens)
         kept = BF16 if slot + 1 == last else F32
 
         def prepare(emit, load, views, results):
             put_rows(results[0], first_back(sizes, load(0)))
             put_columns(results[1], second_back(sizes, load(1)))
             gates = column(load(2)[...], tokens)
-            results[2][...] = slope_of(load(3)[:, columns], gates)
+            results[2][...] = slope_of(load(3)[...], gates)
             results[3][...] = load(4)[...]
 
         task = (
@@ -473,7 +491,7 @@
                 first_of(slot + 1),
                 second_of(slot),
                 gate_of(slot),
-                mixeds[slot],
+                mixeds[slot][moment],
                 grads[moment][slot + 1],
             ],
             [square, square, slim_f32, shape(tokens, kept)],
@@ -509,7 +527,8 @@
         return send, scaled, others
 
     for slot in reversed(range(last)):
-        send, started, _ = step(0, slot, send, started)
+        send, started, others = step(0, slot, send, started, [gate_first(slot + 1)])
+        ((gate_parts[slot + 1],),) = others
 
     def prepare_emit(emit, load, views, results):
         put_rows(results[0], first_back(sizes, load(0)))
@@ -518,20 +537,21 @@
     def prepare_again(emit, load, views, results):
         put_columns(results[0], second_back(sizes, load(0)))
         gates = column(load(1)[...], tokens)
-        results[1][...] = slope_of(load(2)[:, tokens:], gates)
+        results[1][...] = slope_of(load(2)[...], gates)
         results[2][...] = load(3)[...]
 
-    (first_now, grad), (second_now, slope, loss) = merged(
+    (first_now, grad), (second_now, slope, loss), (gate_parts[0],) = merged(
         "window_emit",
         [
             (prepare_emit, [first_of(0), grads[0][0]], [square, slim_f32], [], []),
             (
                 prepare_again,
-                [second_of(last), gate_of(last), mixeds[last], loss],
+                [second_of(last), gate_of(last), mixeds[last][1], loss],
                 [square, slim_f32, slim],
                 [],
                 [],
             ),
+            gate_first(0),
         ],
         [started],
     )

time: 138 us -> 138 us (level)
  Pallas kernels: 37.9 us -> 40 us
  waiting for transfers between devices: 35 us -> 33 us
    pallas_call x20, Pallas kernels: 37.9 us -> 40 us  [call(): pl.pallas_call(kernel, out_shape=[*v_out, *(pltpu.HBM(a.shape, a.dtype) f...]
    all_to_all x9, waiting for transfers between devices: 33 us -> 31 us  [exchange(): lax.all_to_all(shaped, 'tensor', 0, 0, tiled=True).reshape(rows, columns)]
  transfers between devices with their start and end apart: 10 -> 10, of which waited for: 10 -> 10; matrix products, arithmetic and copies ran while one was open for 1% -> 1% of each run, Pallas kernels for 18% -> 19%
where the time goes in v3:
time: 138 us; the launch traced here: 137 us
  starting transfers between devices  60.2 us (44%)
  Pallas kernels  40 us (29%)
  waiting for transfers between devices  33 us (24%)
  between operations  1.65 us (1%)
    all_to_all x9, starting transfers between devices, exchange(): lax.all_to_all(shaped, 'tensor', 0, 0, tiled=True).reshape(rows, columns)  58.9 us
    pallas_call x20, Pallas kernels, call(): pl.pallas_call(kernel, out_shape=[*v_out, *(pltpu.HBM(a.shape, a.dtype) f...  40 us
    all_to_all x9, waiting for transfers between devices, exchange(): lax.all_to_all(shaped, 'tensor', 0, 0, tiled=True).reshape(rows, columns)  31 us
  transfers between devices with their start and end apart: 10, of which 10 were waited for; matrix products, arithmetic and copies ran while one was open for 1% of the time, Pallas kernels for 19%

profile of v3, /device:TPU:2, one launch (start us, length us, event | category | flops | bytes accessed | tf_op | source)
XLA Modules:
  0.0 136.8 jit_solution(3730273356934991129)
XLA Ops:
  0.6 2.2 %open.1 = bf16[512,256]{1,0:T(8,128)(2,1)} custom-call(bf16[1,3,4,128,128]{4,3,2,1,0:T(8,128)(2,1)} %refs_0_.19, bf16[1,2,512,128]{3,2,1,0:T(8,128)(2,1)} %refs_3_.3), custom_call_target="tpu_custom_call" | custom-call | bytes 917504 | tf_op jit(solution)/shard_map/open/pallas_call | solution.py:86
  2.8 16.5 %all-to-all-start = ((bf16[16,32,256]{2,1,0:T(8,128)(2,1)}), bf16[16,32,256]{2,1,0:T(8,128)(2,1)S(1)}, u32[]{:S(2)}, u32[]{:S(2)}) async-start(bf16[16,32,256]{2,1,0:T(8,128)(2,1)} %bitcast.37), calls=%async_computation | async-start | bytes 524288 | tf_op jit(solution)/shard_map/all_to_all | solution.py:250
  20.7 1.8 %prepare_forward_0.1 = (bf16[512,512]{1,0:T(8,128)(2,1)S(1)}, bf16[512,512]{1,0:T(8,128)(2,1)S(1)}, f32[512,128]{1,0:T(8,128)S(1)}, bf16[512,256]{1,0:T(8,128)(2,1)S(1)}) custom-call(bf16[1,3,4,128,128]{4,3,2,1,0:T(8,128)(2,1)} %refs_1_.13, bf16[1,3,4,128,128]{4,3,2,1,0:T(8,128)(2,1)} %refs_0_.19, f32[3,1,512]{2,1,0:T(1,128)} %broadcast_select_fusion.refs_2_.refs_1_.refs_3_, ...), custom_call_target="tpu_custom_call" | custom-call | bytes 1024 | tf_op jit(solution)/shard_map/prepare_forward_0/pallas_call | solution.py:86
  22.5 3.9 %all-to-all-done = bf16[16,32,256]{2,1,0:T(8,128)(2,1)S(1)} async-done(((bf16[16,32,256]{2,1,0:T(8,128)(2,1)}), bf16[16,32,256]{2,1,0:T(8,128)(2,1)S(1)}, u32[]{:S(2)}, u32[]{:S(2)}) %all-to-all-start) | async-done | bytes 262176 | tf_op jit(solution)/shard_map/all_to_all | solution.py:250
  26.4 1.4 %forward_0.1 = (bf16[512,256]{1,0:T(8,128)(2,1)}, bf16[512,256]{1,0:T(8,128)(2,1)}, f32[512,128]{1,0:T(8,128)}, bf16[512,256]{1,0:T(8,128)(2,1)}, f32[512,128]{1,0:T(8,128)}) custom-call(bf16[512,256]{1,0:T(8,128)(2,1)S(1)} %bitcast.29, bf16[512,256]{1,0:T(8,128)(2,1)S(1)} %get-tuple-element.90.refs_1_, f32[512,128]{1,0:T(8,128)S(1)} %get-tuple-element.91.refs_2_, ...), custom_call_target="tpu_custom_call" | custom-call | bytes 3145728 | tf_op jit(solution)/shard_map/forward_0/pallas_call | solution.py:86
  27.8 5.3 %all-to-all-start.1 = ((bf16[16,32,256]{2,1,0:T(8,128)(2,1)}), bf16[16,32,256]{2,1,0:T(8,128)(2,1)S(1)}, u32[]{:S(2)}, u32[]{:S(2)}) async-start(bf16[16,32,256]{2,1,0:T(8,128)(2,1)} %bitcast.38), calls=%async_computation.1 | async-start | bytes 524288 | tf_op jit(solution)/shard_map/all_to_all | solution.py:250
  33.2 1.8 %prepare_forward_1.1 = (bf16[512,512]{1,0:T(8,128)(2,1)S(1)}, bf16[512,512]{1,0:T(8,128)(2,1)S(1)}, f32[512,128]{1,0:T(8,128)S(1)}, bf16[512,256]{1,0:T(8,128)(2,1)S(1)}) custom-call(bf16[1,3,4,128,128]{4,3,2,1,0:T(8,128)(2,1)} %refs_1_.13, bf16[1,3,4,128,128]{4,3,2,1,0:T(8,128)(2,1)} %refs_0_.19, f32[3,1,512]{2,1,0:T(1,128)} %broadcast_select_fusion.refs_2_.refs_1_.refs_3_, ...), custom_call_target="tpu_custom_call" | custom-call | bytes 1024 | tf_op jit(solution)/shard_map/prepare_forward_1/pallas_call | solution.py:86
  34.9 5.8 %all-to-all-done.1 = bf16[16,32,256]{2,1,0:T(8,128)(2,1)S(1)} async-done(((bf16[16,32,256]{2,1,0:T(8,128)(2,1)}), bf16[16,32,256]{2,1,0:T(8,128)(2,1)S(1)}, u32[]{:S(2)}, u32[]{:S(2)}) %all-to-all-start.1) | async-done | bytes 262176 | tf_op jit(solution)/shard_map/all_to_all | solution.py:250
  40.7 1.4 %forward_1.1 = (bf16[512,256]{1,0:T(8,128)(2,1)}, bf16[512,256]{1,0:T(8,128)(2,1)}, f32[512,128]{1,0:T(8,128)}, bf16[512,256]{1,0:T(8,128)(2,1)}, f32[512,128]{1,0:T(8,128)}) custom-call(bf16[512,256]{1,0:T(8,128)(2,1)S(1)} %bitcast.30, bf16[512,256]{1,0:T(8,128)(2,1)S(1)} %get-tuple-element.96.refs_1_, f32[512,128]{1,0:T(8,128)S(1)} %get-tuple-element.97.refs_2_, ...), custom_call_target="tpu_custom_call" | custom-call | bytes 3145728 | tf_op jit(solution)/shard_map/forward_1/pallas_call | solution.py:86
  42.1 5.7 %all-to-all-start.2 = ((bf16[16,32,256]{2,1,0:T(8,128)(2,1)}), bf16[16,32,256]{2,1,0:T(8,128)(2,1)S(1)}, u32[]{:S(2)}, u32[]{:S(2)}) async-start(bf16[16,32,256]{2,1,0:T(8,128)(2,1)} %bitcast.39), calls=%async_computation.2 | async-start | bytes 524288 | tf_op jit(solution)/shard_map/all_to_all | solution.py:250
  47.9 1.6 %prepare_turn.1 = (bf16[512,512]{1,0:T(8,128)(2,1)S(1)}, bf16[512,512]{1,0:T(8,128)(2,1)S(1)}, f32[512,128]{1,0:T(8,128)S(1)}, bf16[512,128]{1,0:T(8,128)(2,1)S(1)}) custom-call(bf16[1,3,4,128,128]{4,3,2,1,0:T(8,128)(2,1)} %refs_1_.13, f32[3,1,512]{2,1,0:T(1,128)} %broadcast_select_fusion.refs_2_.refs_1_.refs_3_, bf16[1,512,128]{2,1,0:T(8,128)(2,1)} %refs_4_.3, ...), custom_call_target="tpu_custom_call" | custom-call | bytes 1024 | tf_op jit(solution)/shard_map/prepare_turn/pallas_call | solution.py:86
  49.5 5.2 %all-to-all-done.2 = bf16[16,32,256]{2,1,0:T(8,128)(2,1)S(1)} async-done(((bf16[16,32,256]{2,1,0:T(8,128)(2,1)}), bf16[16,32,256]{2,1,0:T(8,128)(2,1)S(1)}, u32[]{:S(2)}, u32[]{:S(2)}) %all-to-all-start.2) | async-done | bytes 262176 | tf_op jit(solution)/shard_map/all_to_all | solution.py:250
  54.7 1.3 turn.1
  56.0 5.4 %all-to-all-start.3 = ((bf16[16,32,128]{2,1,0:T(8,128)(2,1)}), bf16[16,32,128]{2,1,0:T(8,128)(2,1)S(1)}, u32[]{:S(2)}, u32[]{:S(2)}) async-start(bf16[16,32,128]{2,1,0:T(8,128)(2,1)} %bitcast.45), calls=%async_computation.3 | async-start | bytes 262144 | tf_op jit(solution)/shard_map/all_to_all | solution.py:250
  61.4 2.8 %window_0_1.1 = (bf16[512,512]{1,0:T(8,128)(2,1)S(1)}, bf16[512,512]{1,0:T(8,128)(2,1)S(1)}, f32[512,128]{1,0:T(8,128)S(1)}, bf16[512,128]{1,0:T(8,128)(2,1)S(1)}, f32[1,512]{1,0:T(1,128)}) custom-call(bf16[1,3,4,128,128]{4,3,2,1,0:T(8,128)(2,1)} %refs_0_.19, bf16[1,3,4,128,128]{4,3,2,1,0:T(8,128)(2,1)} %refs_1_.13, ...), custom_call_target="tpu_custom_call" | custom-call | bytes 1024 | tf_op jit(solution)/shard_map/window_0_1/pallas_call | solution.py:86
  64.1 3.6 %all-to-all-done.3 = bf16[16,32,128]{2,1,0:T(8,128)(2,1)S(1)} async-done(((bf16[16,32,128]{2,1,0:T(8,128)(2,1)}), bf16[16,32,128]{2,1,0:T(8,128)(2,1)S(1)}, u32[]{:S(2)}, u32[]{:S(2)}) %all-to-all-start.3) | async-done | bytes 131104 | tf_op jit(solution)/shard_map/all_to_all | solution.py:250
  69.0 5.1 %all-to-all-start.4 = ((bf16[16,32,128]{2,1,0:T(8,128)(2,1)}), bf16[16,32,128]{2,1,0:T(8,128)(2,1)S(1)}, u32[]{:S(2)}, u32[]{:S(2)}) async-start(bf16[16,32,128]{2,1,0:T(8,128)(2,1)} %bitcast.42), calls=%async_computation.4 | async-start | bytes 262144 | tf_op jit(solution)/shard_map/all_to_all | solution.py:250
  74.1 2.8 %window_0_0.1 = (bf16[512,512]{1,0:T(8,128)(2,1)S(1)}, bf16[512,512]{1,0:T(8,128)(2,1)S(1)}, f32[512,128]{1,0:T(8,128)S(1)}, f32[512,128]{1,0:T(8,128)S(1)}, f32[1,512]{1,0:T(1,128)}) custom-call(bf16[1,3,4,128,128]{4,3,2,1,0:T(8,128)(2,1)} %refs_0_.19, bf16[1,3,4,128,128]{4,3,2,1,0:T(8,128)(2,1)} %refs_1_.13, ...), custom_call_target="tpu_custom_call" | custom-call | bytes 1024 | tf_op jit(solution)/shard_map/window_0_0/pallas_call | solution.py:86
  76.9 3.6 %all-to-all-done.4 = bf16[16,32,128]{2,1,0:T(8,128)(2,1)S(1)} async-done(((bf16[16,32,128]{2,1,0:T(8,128)(2,1)}), bf16[16,32,128]{2,1,0:T(8,128)(2,1)S(1)}, u32[]{:S(2)}, u32[]{:S(2)}) %all-to-all-start.4) | async-done | bytes 131104 | tf_op jit(solution)/shard_map/all_to_all | solution.py:250
  81.8 5.2 %all-to-all-start.5 = ((bf16[16,32,128]{2,1,0:T(8,128)(2,1)}), bf16[16,32,128]{2,1,0:T(8,128)(2,1)S(1)}, u32[]{:S(2)}, u32[]{:S(2)}) async-start(bf16[16,32,128]{2,1,0:T(8,128)(2,1)} %bitcast.44), calls=%async_computation.5 | async-start | bytes 262144 | tf_op jit(solution)/shard_map/all_to_all | solution.py:250
  87.6 2.8 %window_emit.1 = (bf16[512,512]{1,0:T(8,128)(2,1)S(1)}, f32[512,128]{1,0:T(8,128)S(1)}, bf16[512,512]{1,0:T(8,128)(2,1)S(1)}, f32[512,128]{1,0:T(8,128)S(1)}, bf...) custom-call(bf16[1,3,4,128,128]{4,3,2,1,0:T(8,128)(2,1)} %refs_0_.19, f32[512,128]{1,0:T(8,128)} %get-tuple-element.123.refs_1_, ...), custom_call_target="tpu_custom_call" | custom-call | bytes 1024 | tf_op jit(solution)/shard_map/window_emit/pallas_call | solution.py:86
  90.5 2.9 %all-to-all-done.5 = bf16[16,32,128]{2,1,0:T(8,128)(2,1)S(1)} async-done(((bf16[16,32,128]{2,1,0:T(8,128)(2,1)}), bf16[16,32,128]{2,1,0:T(8,128)(2,1)S(1)}, u32[]{:S(2)}, u32[]{:S(2)}) %all-to-all-start.5) | async-done | bytes 131104 | tf_op jit(solution)/shard_map/all_to_all | solution.py:250
  95.0 1.9 %collective-permute-done.refs_0_ = bf16[512,128]{1,0:T(8,128)(2,1)S(1)} collective-permute-done((bf16[512,128]{1,0:T(8,128)(2,1)S(1)}, bf16[512,128]{1,0:T(8,128)(2,1)S(1)}, u32[]{:S(2)}, u32[]{:S(2)}) %collective-permute-start) | collective-permute-done | bytes 131104 | tf_op jit(solution)/shard_map/ppermute | solution.py:567
  98.0 5.1 %all-to-all-start.6 = ((bf16[16,32,128]{2,1,0:T(8,128)(2,1)}), bf16[16,32,128]{2,1,0:T(8,128)(2,1)S(1)}, u32[]{:S(2)}, u32[]{:S(2)}) async-start(bf16[16,32,128]{2,1,0:T(8,128)(2,1)} %bitcast.43), calls=%async_computation.6 | async-start | bytes 262144 | tf_op jit(solution)/shard_map/all_to_all | solution.py:250
  103.7 3.8 %window_1_1.1 = (bf16[512,512]{1,0:T(8,128)(2,1)S(1)}, bf16[512,512]{1,0:T(8,128)(2,1)S(1)}, f32[512,128]{1,0:T(8,128)S(1)}, bf16[512,128]{1,0:T(8,128)(2,1)S(1)...) custom-call(bf16[1,3,4,128,128]{4,3,2,1,0:T(8,128)(2,1)} %refs_0_.19, ...), custom_call_target="tpu_custom_call" | custom-call | bytes 1024 | tf_op jit(solution)/shard_map/window_1_1/pallas_call | solution.py:86
  107.5 1.9 %all-to-all-done.6 = bf16[16,32,128]{2,1,0:T(8,128)(2,1)S(1)} async-done(((bf16[16,32,128]{2,1,0:T(8,128)(2,1)}), bf16[16,32,128]{2,1,0:T(8,128)(2,1)S(1)}, u32[]{:S(2)}, u32[]{:S(2)}) %all-to-all-start.6) | async-done | bytes 131104 | tf_op jit(solution)/shard_map/all_to_all | solution.py:250
  110.7 5.3 %all-to-all-start.7 = ((bf16[16,32,128]{2,1,0:T(8,128)(2,1)}), bf16[16,32,128]{2,1,0:T(8,128)(2,1)S(1)}, u32[]{:S(2)}, u32[]{:S(2)}) async-start(bf16[16,32,128]{2,1,0:T(8,128)(2,1)} %bitcast.41), calls=%async_computation.7 | async-start | bytes 262144 | tf_op jit(solution)/shard_map/all_to_all | solution.py:250
  116.0 4.4 %window_1_0.1 = (bf16[512,512]{1,0:T(8,128)(2,1)S(1)}, bf16[512,512]{1,0:T(8,128)(2,1)S(1)}, f32[512,128]{1,0:T(8,128)S(1)}, f32[512,128]{1,0:T(8,128)S(1)}, f32...) custom-call(bf16[1,3,4,128,128]{4,3,2,1,0:T(8,128)(2,1)} %refs_0_.19, ...), custom_call_target="tpu_custom_call", output_to_operand_aliasing={{4}: (15, {}), {5}: (16, {})} | custom-call | bytes 1024 | tf_op jit(solution)/shard_map/window_1_0/pallas_call | solution.py:86
  120.5 1.9 %all-to-all-done.7 = bf16[16,32,128]{2,1,0:T(8,128)(2,1)S(1)} async-done(((bf16[16,32,128]{2,1,0:T(8,128)(2,1)}), bf16[16,32,128]{2,1,0:T(8,128)(2,1)S(1)}, u32[]{:S(2)}, u32[]{:S(2)}) %all-to-all-start.7) | async-done | bytes 131104 | tf_op jit(solution)/shard_map/all_to_all | solution.py:250
  123.7 5.3 %all-to-all-start.8 = ((bf16[16,32,128]{2,1,0:T(8,128)(2,1)}), bf16[16,32,128]{2,1,0:T(8,128)(2,1)S(1)}, u32[]{:S(2)}, u32[]{:S(2)}) async-start(bf16[16,32,128]{2,1,0:T(8,128)(2,1)} %bitcast.40), calls=%async_computation.8 | async-start | bytes 262144 | tf_op jit(solution)/shard_map/all_to_all | solution.py:250
  129.0 4.3 %window_close.1 = (bf16[512,512]{1,0:T(8,128)(2,1)S(1)}, f32[512,128]{1,0:T(8,128)S(1)}, bf16[512,512]{1,0:T(8,128)(2,1)S(1)}, bf16[512,128]{1,0:T(8,128)(2,1)S(...) custom-call(bf16[1,3,4,128,128]{4,3,2,1,0:T(8,128)(2,1)} %refs_0_.19, ...), custom_call_target="tpu_custom_call", output_to_operand_aliasing={{5}: (14, {}), {6}: (15, {}), {7}: (16, {})} | custom-call | bytes 1024 | tf_op jit(solution)/shard_map/window_close/pallas_call | solution.py:86
  133.3 2.1 %all-to-all-done.8 = bf16[16,32,128]{2,1,0:T(8,128)(2,1)S(1)} async-done(((bf16[16,32,128]{2,1,0:T(8,128)(2,1)}), bf16[16,32,128]{2,1,0:T(8,128)(2,1)S(1)}, u32[]{:S(2)}, u32[]{:S(2)}) %all-to-all-start.8) | async-done | bytes 131104 | tf_op jit(solution)/shard_map/all_to_all | solution.py:250
  (17 shorter events, 11.0 us)
Async XLA Ops:
  2.8 17.2 %copy-start.1 = (f32[1,3,512]{2,0,1:T(1,128)S(1)}, f32[1,3,512]{2,0,1:T(1,128)}, u32[]{:S(2)}) copy-start(f32[1,3,512]{2,0,1:T(1,128)} %param.12) | copy-start | bytes 18436
  2.8 23.6 %all-to-all-start = ((bf16[16,32,256]{2,1,0:T(8,128)(2,1)}), bf16[16,32,256]{2,1,0:T(8,128)(2,1)S(1)}, u32[]{:S(2)}, u32[]{:S(2)}) async-start(bf16[16,32,256]{2,1,0:T(8,128)(2,1)} %bitcast.37), calls=%async_computation | async-start | bytes 524288 | tf_op jit(solution)/shard_map/all_to_all | solution.py:250
  27.8 12.9 %all-to-all-start.1 = ((bf16[16,32,256]{2,1,0:T(8,128)(2,1)}), bf16[16,32,256]{2,1,0:T(8,128)(2,1)S(1)}, u32[]{:S(2)}, u32[]{:S(2)}) async-start(bf16[16,32,256]{2,1,0:T(8,128)(2,1)} %bitcast.38), calls=%async_computation.1 | async-start | bytes 524288 | tf_op jit(solution)/shard_map/all_to_all | solution.py:250
  42.1 12.5 %all-to-all-start.2 = ((bf16[16,32,256]{2,1,0:T(8,128)(2,1)}), bf16[16,32,256]{2,1,0:T(8,128)(2,1)S(1)}, u32[]{:S(2)}, u32[]{:S(2)}) async-start(bf16[16,32,256]{2,1,0:T(8,128)(2,1)} %bitcast.39), calls=%async_computation.2 | async-start | bytes 524288 | tf_op jit(solution)/shard_map/all_to_all | solution.py:250
  56.0 11.8 %all-to-all-start.3 = ((bf16[16,32,128]{2,1,0:T(8,128)(2,1)}), bf16[16,32,128]{2,1,0:T(8,128)(2,1)S(1)}, u32[]{:S(2)}, u32[]{:S(2)}) async-start(bf16[16,32,128]{2,1,0:T(8,128)(2,1)} %bitcast.45), calls=%async_computation.3 | async-start | bytes 262144 | tf_op jit(solution)/shard_map/all_to_all | solution.py:250
  69.0 11.5 %all-to-all-start.4 = ((bf16[16,32,128]{2,1,0:T(8,128)(2,1)}), bf16[16,32,128]{2,1,0:T(8,128)(2,1)S(1)}, u32[]{:S(2)}, u32[]{:S(2)}) async-start(bf16[16,32,128]{2,1,0:T(8,128)(2,1)} %bitcast.42), calls=%async_computation.4 | async-start | bytes 262144 | tf_op jit(solution)/shard_map/all_to_all | solution.py:250
  81.8 5.2 %copy-start = (bf16[1,512,128]{2,1,0:T(8,128)(2,1)S(1)}, bf16[1,512,128]{2,1,0:T(8,128)(2,1)}, u32[]{:S(2)}) copy-start(bf16[1,512,128]{2,1,0:T(8,128)(2,1)} %param.9) | copy-start | bytes 393220
  81.8 11.6 %all-to-all-start.5 = ((bf16[16,32,128]{2,1,0:T(8,128)(2,1)}), bf16[16,32,128]{2,1,0:T(8,128)(2,1)S(1)}, u32[]{:S(2)}, u32[]{:S(2)}) async-start(bf16[16,32,128]{2,1,0:T(8,128)(2,1)} %bitcast.44), calls=%async_computation.5 | async-start | bytes 262144 | tf_op jit(solution)/shard_map/all_to_all | solution.py:250
  93.7 3.2 %collective-permute-start = (bf16[512,128]{1,0:T(8,128)(2,1)S(1)}, bf16[512,128]{1,0:T(8,128)(2,1)S(1)}, u32[]{:S(2)}, u32[]{:S(2)}) collective-permute-start(bf16[512,128]{1,0:T(8,128)(2,1)S(1)} %emit.1), channel_id=1, source_target_pairs={{16,0},{32,16},{48,32},{64,48},{80,64},{96,80},{112,96},{128,112},... | collective-permute-start | bytes 393224 | tf_op jit(solution)/shard_map/ppermute | solution.py:567
  98.0 11.5 %all-to-all-start.6 = ((bf16[16,32,128]{2,1,0:T(8,128)(2,1)}), bf16[16,32,128]{2,1,0:T(8,128)(2,1)S(1)}, u32[]{:S(2)}, u32[]{:S(2)}) async-start(bf16[16,32,128]{2,1,0:T(8,128)(2,1)} %bitcast.43), calls=%async_computation.6 | async-start | bytes 262144 | tf_op jit(solution)/shard_map/all_to_all | solution.py:250
  110.7 11.7 %all-to-all-start.7 = ((bf16[16,32,128]{2,1,0:T(8,128)(2,1)}), bf16[16,32,128]{2,1,0:T(8,128)(2,1)S(1)}, u32[]{:S(2)}, u32[]{:S(2)}) async-start(bf16[16,32,128]{2,1,0:T(8,128)(2,1)} %bitcast.41), calls=%async_computation.7 | async-start | bytes 262144 | tf_op jit(solution)/shard_map/all_to_all | solution.py:250
  123.7 11.7 %all-to-all-start.8 = ((bf16[16,32,128]{2,1,0:T(8,128)(2,1)}), bf16[16,32,128]{2,1,0:T(8,128)(2,1)S(1)}, u32[]{:S(2)}, u32[]{:S(2)}) async-start(bf16[16,32,128]{2,1,0:T(8,128)(2,1)} %bitcast.40), calls=%async_computation.8 | async-start | bytes 262144 | tf_op jit(solution)/shard_map/all_to_all | solution.py:250
